TPU v7x, 256 devices: a whole 4x4x8 slice. The times are simulated.
256 devices in a mesh: lon: 16 (over x, y_lo, core), dates: 16 (over z, y_hi).
Axes of the slice: x: 4, y: 4 (y_hi: 2, y_lo: 2; y = y_hi * 2 + y_lo), z: 8, core: 2. Of those that a mesh axis runs over, the one named last changes fastest.
Arguments:
- features: bfloat16 [16, 4096, 1024], P('dates', 'lon'), may hold values from -24 to 24
- w_qkv: bfloat16 [1024, 3072], replicated, may hold values from -2 to 2
- grad_out: bfloat16 [16, 4096, 1024], P('dates', 'lon'), may hold values from -6 to 6
- positions: int32 [16, 4096], P('dates', 'lon'), may hold values from 0 to 4095, as said below
- block_list: int32 [16, 5], P('dates'), may hold values from -2 to 2, as said below
Outputs:
- attn_out: bfloat16 [16, 4096, 1024], P('dates', 'lon')
- grad_x: bfloat16 [16, 4096, 1024], P('dates', 'lon')
- grad_w: float32 [1024, 3072], P('dates', 'lon')
Inputs may be any that keep to these rules, and one draw needn't show every extreme that they name: `positions`: positions never fall along a sample's row. `block_list`: each sample's list holds 0 and every offset from -r to r for its reach r of 0 to 2; other entries are 0; some sample has reach 2.
All inputs are finite; a program needn't handle non-finite values.
Results may differ from a plain program's by a relative error of at most 0.034.
Values may be sent and summed in bfloat16 or wider, within the bound.
A program may use at most 128 MiB of HBM per device.

v0:
```python
import jax
import jax.numpy as jnp
from jax import lax
from jax.sharding import PartitionSpec as P

HEADS = 16
W_MAX = 2


INTERP = 0.25
BASE = 10000.0
NEG_FILL = -1e30


def from_behind(value, axis, by):
    size = lax.axis_size(axis)
    return lax.ppermute(value, axis, [(i, (i + by) % size) for i in range(size)])


def rope_tables(row_positions, head_dim):
    pair_index = jnp.arange(head_dim // 2, dtype=jnp.float32)
    frequency = INTERP * BASE ** (-2.0 * pair_index / head_dim)
    angles = row_positions.astype(jnp.float32)[..., None] * frequency
    return (jnp.cos(angles)[..., None, :], jnp.sin(angles)[..., None, :])


def rotate(values, cosine, sine_table):
    half_dim = values.shape[-1] // 2
    first_half = values[..., :half_dim]
    second_half = values[..., half_dim:]
    return jnp.concatenate(
        [
            first_half * cosine - second_half * sine_table,
            first_half * sine_table + second_half * cosine,
        ],
        axis=-1,
    )


def unrotate(values, cosine, sine_table):
    half_dim = values.shape[-1] // 2
    first_half = values[..., :half_dim]
    second_half = values[..., half_dim:]
    return jnp.concatenate(
        [
            first_half * cosine + second_half * sine_table,
            second_half * cosine - first_half * sine_table,
        ],
        axis=-1,
    )


def head_major(blocks):
    return jnp.transpose(blocks, (4, 0, 1, 2, 3, 5))


def block_scores(single_query, single_key, used_slots, score_scale):
    raw_scores = (
        jnp.einsum("mch,emih->mcei", single_query, single_key, preferred_element_type=jnp.float32)
        * score_scale
    )
    return jnp.where(used_slots[:, None, :, None], raw_scores, NEG_FILL)


def per_device(features, w_qkv, grad_out, positions, block_list):
    batch, lon_dev, width = features.shape
    head_dim = width // HEADS
    score_scale = head_dim ** (-0.5)
    offsets = jnp.arange(-W_MAX, W_MAX + 1, dtype=jnp.int32)
    used_slots = jnp.any(block_list[:, :, None] == offsets[None, None, :], axis=1)
    mask = used_slots[:, None, :, None]
    projected = jnp.einsum("bld,de->ble", features, w_qkv, preferred_element_type=jnp.float32)
    cosine, sine_table = rope_tables(positions, head_dim)
    head_shape = (batch, lon_dev, HEADS, head_dim)
    query = rotate(projected[..., :width].reshape(head_shape), cosine, sine_table).astype(
        jnp.bfloat16
    )
    key_row_stack = rotate(
        projected[..., width : 2 * width].reshape(head_shape), cosine, sine_table
    ).astype(jnp.bfloat16)
    values = projected[..., 2 * width :].astype(jnp.bfloat16).reshape(head_shape)
    key_value = jnp.stack([key_row_stack, values])
    lower_blocks = []
    moving = key_value
    for distance in range(W_MAX):
        moving = from_behind(moving, "lon", 1)
        lower_blocks.append(moving)
    upper_blocks = []
    moving = key_value
    for distance in range(W_MAX):
        moving = from_behind(moving, "lon", -1)
        upper_blocks.append(moving)
    stacked = jnp.stack(lower_blocks[::-1] + [key_value] + upper_blocks)
    query_heads = jnp.transpose(query, (2, 0, 1, 3))
    upstream = jnp.transpose(grad_out.reshape(head_shape), (2, 0, 1, 3))

    def forward_head(items):
        single_query, single_pair = items
        scores = block_scores(single_query, single_pair[:, 0], used_slots, score_scale)
        row_max = jnp.max(scores, axis=(2, 3), keepdims=True)
        exp_scores = jnp.where(mask, jnp.exp(scores - row_max), 0.0)
        totals = jnp.sum(exp_scores, axis=(2, 3), keepdims=True)
        reduced_probabilities = (exp_scores / totals).astype(jnp.bfloat16)
        out_one = jnp.einsum(
            "iexf,xifl->iel",
            reduced_probabilities,
            single_pair[:, 1],
            preferred_element_type=jnp.float32,
        ).astype(jnp.bfloat16)
        return (out_one, row_max, totals)

    out_heads, max_heads, total_heads = lax.map(forward_head, (query_heads, head_major(stacked)))
    attn_out = jnp.transpose(out_heads, (1, 2, 0, 3)).reshape(batch, lon_dev, width)
    again_lower = []
    moving = key_value
    for distance in range(W_MAX):
        moving = from_behind(moving, "lon", 1)
        again_lower.append(moving)
    again_upper = []
    moving = key_value
    for distance in range(W_MAX):
        moving = from_behind(moving, "lon", -1)
        again_upper.append(moving)
    stacked_back = jnp.stack(again_lower[::-1] + [key_value] + again_upper)

    def backward_head(items):
        single_query, single_pair, out_one, row_max, totals, single_gradient = items
        scores = block_scores(single_query, single_pair[:, 0], used_slots, score_scale)
        attn_probs = jnp.where(mask, jnp.exp(scores - row_max), 0.0) / totals
        reduced_probabilities = attn_probs.astype(jnp.bfloat16)
        row_delta = jnp.sum(
            single_gradient.astype(jnp.float32) * out_one.astype(jnp.float32), axis=-1
        )
        dprobs = jnp.einsum(
            "mch,emih->mcei", single_gradient, single_pair[:, 1], preferred_element_type=jnp.float32
        )
        score_gradient = (attn_probs * (dprobs - row_delta[:, :, None, None])).astype(jnp.bfloat16)
        dquery = score_scale * jnp.einsum(
            "iexf,xifl->iel", score_gradient, single_pair[:, 0], preferred_element_type=jnp.float32
        )
        key_grads = score_scale * jnp.einsum(
            "pfxg,pfo->xpgo", score_gradient, single_query, preferred_element_type=jnp.float32
        )
        value_grads = jnp.einsum(
            "pfxg,pfo->xpgo",
            reduced_probabilities,
            single_gradient,
            preferred_element_type=jnp.float32,
        )
        return (dquery, jnp.stack([key_grads, value_grads], axis=1))

    dquery_heads, part_heads = lax.map(
        backward_head,
        (query_heads, head_major(stacked_back), out_heads, max_heads, total_heads, upstream),
    )
    parts = jnp.transpose(part_heads, (1, 2, 3, 4, 0, 5))
    lower_sum = parts[0]
    for distance in range(W_MAX - 1, -1, -1):
        lower_sum = from_behind(lower_sum, "lon", -1)
        if distance > 0:
            lower_sum = lower_sum + parts[W_MAX - distance]
    upper_sum = parts[2 * W_MAX]
    for distance in range(W_MAX - 1, -1, -1):
        upper_sum = from_behind(upper_sum, "lon", 1)
        if distance > 0:
            upper_sum = upper_sum + parts[W_MAX + distance]
    grads_home = parts[W_MAX] + lower_sum + upper_sum
    dquery_full = unrotate(jnp.transpose(dquery_heads, (1, 2, 0, 3)), cosine, sine_table)
    dkey_full = unrotate(grads_home[0], cosine, sine_table)
    flat_shape = (batch, lon_dev, width)
    dqkv = jnp.concatenate(
        [
            dquery_full.reshape(flat_shape),
            dkey_full.reshape(flat_shape),
            grads_home[1].reshape(flat_shape),
        ],
        axis=-1,
    ).astype(jnp.bfloat16)
    grad_x = jnp.einsum("ble,de->bld", dqkv, w_qkv, preferred_element_type=jnp.float32).astype(
        jnp.bfloat16
    )
    factor = (batch * lax.axis_size("dates") * lon_dev * lax.axis_size("lon")) ** (-0.5)
    feat_flat = features.reshape(batch * lon_dev, width)
    dqkv_flat = dqkv.reshape(batch * lon_dev, 3 * width)
    weight_term = (
        jnp.einsum("td,te->de", feat_flat, dqkv_flat, preferred_element_type=jnp.float32) * factor
    )
    own_cols = lax.psum_scatter(weight_term, "lon", scatter_dimension=1, tiled=True)
    grad_w = lax.psum_scatter(own_cols, "dates", scatter_dimension=0, tiled=True)
    return (attn_out, grad_x, grad_w)


def solution(mesh):
    return jax.shard_map(
        per_device,
        mesh=mesh,
        in_specs=(
            P("dates", "lon", None),
            P(),
            P("dates", "lon", None),
            P("dates", "lon"),
            P("dates", None),
        ),
        out_specs=(P("dates", "lon", None), P("dates", "lon", None), P("dates", "lon")),
        check_vma=False,
    )
```

profile of v0, /device:TPU:7, one launch (start us, length us, event | category | flops | bytes accessed | tf_op | source)
XLA Modules:
  0.0 636.0 jit_solution(10059095756537417981)
XLA Ops:
  8.2 4.6 convolution_bitcast_fusion.3
  13.7 1.1 fusion.48
  15.1 1.2 copy.64
  16.4 1.6 copy.62
  18.1 1.1 fusion.42
  20.0 1.2 pad_maximum_fusion.1
  21.2 1.9 collective-permute-start
  23.0 23.0 %collective-permute-done = bf16[2,1,256,16,64]{2,4,3,0,1:T(8,128)(2,1)} collective-permute-done((bf16[2,1,256,16,64]{2,4,3,0,1:T(8,128)(2,1)S(1)}, bf16[2,1,256,16,64]{2,4,3,0,1:T(8,128)(2,1)}, u32[]{:S(2)}, u32[]{:S(2)}) %collective-permute-start) | collective-permute-done | bytes 1048608 | tf_op jit(solution)/shard_map/ppermute | solution.py:17
  46.0 2.6 collective-permute-start.1
  48.8 1.1 maximum_bitcast_fusion.1
  49.9 9.0 %collective-permute-done.2 = bf16[2,1,256,16,64]{2,4,3,1,0:T(8,128)(2,1)} collective-permute-done((bf16[2,1,256,16,64]{2,4,3,1,0:T(8,128)(2,1)}, bf16[2,1,256,16,64]{2,4,3,1,0:T(8,128)(2,1)}, u32[]{:S(2)}, u32[]{:S(2)}) %collective-permute-start.2) | collective-permute-done | bytes 1048608 | tf_op jit(solution)/shard_map/ppermute | solution.py:17
  58.9 12.3 %collective-permute-done.1 = bf16[2,1,256,16,64]{2,4,3,0,1:T(8,128)(2,1)} collective-permute-done((bf16[2,1,256,16,64]{2,4,3,0,1:T(8,128)(2,1)}, bf16[2,1,256,16,64]{2,4,3,0,1:T(8,128)(2,1)}, u32[]{:S(2)}, u32[]{:S(2)}) %collective-permute-start.1) | collective-permute-done | bytes 1048608 | tf_op jit(solution)/shard_map/ppermute | solution.py:17
  71.3 1.3 bitcast_dynamic-update-slice_fusion.4
  72.6 1.3 bitcast_dynamic-update-slice_fusion.3
  74.0 1.3 bitcast_dynamic-update-slice_fusion.1
  75.4 2.8 copy.67
  78.3 34.3 %while.26 = (s32[]{:T(128)}, bf16[16,1,256,64]{2,3,1,0:T(8,128)(2,1)S(1)}, f32[16,1,256,1,1]{2,4,3,1,0:T(1,128)S(1)}, f32[16,1,256,1,1]{2,4,3,1,0:T(1,128)S(1)},...) while((s32[]{:T(128)}, ...), condition=%wide.region_4.5_spmd, body=%wide.region_1.4_spmd.sunk | while | flops 87178752 | bytes 4991098 | solution.py:112
  112.5 58.6 %while.27 = (s32[]{:T(128)}, f32[16,1,256,64]{2,3,1,0:T(8,128)S(1)}, f32[16,5,2,1,256,64]{4,5,0,2,3,1:T(8,128)}, pred[1,1,5,1]{2,3,1,0:T(4,128)(4,1)S(1)}, pred[...) while((s32[]{:T(128)}, ...), condition=%wide.region_7.8_spmd, body=%wide.region_5.7_spmd.sunk | while | flops 212991744 | bytes 9282721 | solution.py:152
  112.6 1.0 dynamic-slice_bitcast_fusion.5
  116.3 1.0 dynamic-slice_bitcast_fusion.5
  119.9 1.0 dynamic-slice_bitcast_fusion.5
  123.6 1.0 dynamic-slice_bitcast_fusion.5
  127.2 1.0 dynamic-slice_bitcast_fusion.5
  130.8 1.0 dynamic-slice_bitcast_fusion.5
  134.5 1.0 dynamic-slice_bitcast_fusion.5
  141.8 1.0 dynamic-slice_bitcast_fusion.5
  145.5 1.0 dynamic-slice_bitcast_fusion.5
  149.2 1.0 dynamic-slice_bitcast_fusion.5
  152.9 1.0 dynamic-slice_bitcast_fusion.5
  156.5 1.0 dynamic-slice_bitcast_fusion.5
  160.2 1.0 dynamic-slice_bitcast_fusion.5
  163.9 1.0 dynamic-slice_bitcast_fusion.5
  167.5 1.0 dynamic-slice_bitcast_fusion.5
  171.2 2.8 slice_bitcast_fusion.12
  174.1 2.6 collective-permute-start.6
  176.6 46.1 %collective-permute-done.4 = f32[2,1,256,16,64]{2,4,3,0,1:T(8,128)S(1)} collective-permute-done((f32[2,1,256,16,64]{2,4,3,0,1:T(8,128)S(1)}, f32[2,1,256,16,64]{2,4,3,0,1:T(8,128)S(1)}, u32[]{:S(2)}, u32[]{:S(2)}) %collective-permute-start.4) | collective-permute-done | bytes 2097184 | tf_op jit(solution)/shard_map/ppermute | solution.py:17
  222.7 2.0 fusion.35
  225.0 7.3 %collective-permute-done.6 = f32[2,1,256,16,64]{2,4,3,0,1:T(8,128)S(1)} collective-permute-done((f32[2,1,256,16,64]{2,4,3,0,1:T(8,128)S(1)}, f32[2,1,256,16,64]{2,4,3,0,1:T(8,128)S(1)}, u32[]{:S(2)}, u32[]{:S(2)}) %collective-permute-start.6) | collective-permute-done | bytes 2097184 | tf_op jit(solution)/shard_map/ppermute | solution.py:17
  232.3 1.9 fusion.34
  234.3 2.6 collective-permute-start.7
  236.8 36.1 %collective-permute-done.5 = f32[2,1,256,16,64]{2,4,3,0,1:T(8,128)S(1)} collective-permute-done((f32[2,1,256,16,64]{2,4,3,0,1:T(8,128)S(1)}, f32[2,1,256,16,64]{2,4,3,0,1:T(8,128)S(1)}, u32[]{:S(2)}, u32[]{:S(2)}) %collective-permute-start.5) | collective-permute-done | bytes 2097184 | tf_op jit(solution)/shard_map/ppermute | solution.py:17
  272.9 2.1 fusion.38
  275.6 6.3 multiply_bitcast_fusion
  282.0 143.5 %reduce-scatter.5.cloned.1.call-done = f32[1024,192]{0,1:T(8,128)} async-done(((f32[1024,3072]{0,1:T(8,128)}), f32[1024,192]{0,1:T(8,128)}) %reduce-scatter.5.cloned.1.call-update) | async-done | bytes 786448 | tf_op jit(solution)/shard_map/reduce_scatter | solution.py:188
  425.4 2.5 copy.79
  427.9 1.0 copy.76
  428.9 5.4 fusion.39
  434.3 194.9 %reduce-scatter.7.cloned.1.call-done = f32[64,192]{1,0:T(8,128)} async-done(((f32[1024,192]{1,0:T(8,128)}), f32[64,192]{1,0:T(8,128)}) %reduce-scatter.7.cloned.1.call-update) | async-done | bytes 49168
  (256 shorter events, 81.4 us)
Async XLA Ops:
  7.2 1.0 copy-start
  7.2 418.2 %reduce-scatter.5.cloned.1.call-start = ((), (), s32[]{:S(2)}) async-start(), calls=%async_computation.2 | async-start | bytes 13369344 | tf_op jit(solution)/shard_map/reduce_scatter | solution.py:188
  13.7 1.1 copy-start.7
  19.3 0.7 copy-start.1
  19.3 29.3 %copy-start.6 = (bf16[1,256,1024]{2,1,0:T(8,128)(2,1)S(1)}, bf16[1,256,1024]{2,1,0:T(8,128)(2,1)}, u32[]{:S(2)}) copy-start(bf16[1,256,1024]{2,1,0:T(8,128)(2,1)} %param.11) | copy-start | bytes 1572868
  20.0 38.9 %copy-start.8 = (s32[1,5]{1,0:T(1,128)S(1)}, s32[1,5]{1,0:T(1,128)}, u32[]{:S(2)}) copy-start(s32[1,5]{1,0:T(1,128)} %param.13) | copy-start | bytes 64
  21.2 24.8 %collective-permute-start = (bf16[2,1,256,16,64]{2,4,3,0,1:T(8,128)(2,1)S(1)}, bf16[2,1,256,16,64]{2,4,3,0,1:T(8,128)(2,1)}, u32[]{:S(2)}, u32[]{:S(2)}) collective-permute-start(bf16[2,1,256,16,64]{2,4,3,0,1:T(8,128)(2,1)S(1)} %get-tuple-element.255), channel_id=1, source_target_pairs={{0,16},{16,32},{32,48},{48,64},{64,80},{80,96},{96,112},{112,128},... | collective-permute-start | bytes 3145736 | tf_op jit(solution)/shard_map/ppermute | solution.py:17
  23.0 35.8 %collective-permute-start.2 = (bf16[2,1,256,16,64]{2,4,3,1,0:T(8,128)(2,1)}, bf16[2,1,256,16,64]{2,4,3,1,0:T(8,128)(2,1)}, u32[]{:S(2)}, u32[]{:S(2)}) collective-permute-start(bf16[2,1,256,16,64]{2,4,3,1,0:T(8,128)(2,1)} %get-tuple-element.254), channel_id=1, source_target_pairs={{0,240},{16,0},{32,16},{48,32},{64,48},{80,64},{96,80},{112,96},{1... | collective-permute-start | bytes 3145736 | tf_op jit(solution)/shard_map/ppermute | solution.py:17
  46.0 25.3 %collective-permute-start.1 = (bf16[2,1,256,16,64]{2,4,3,0,1:T(8,128)(2,1)}, bf16[2,1,256,16,64]{2,4,3,0,1:T(8,128)(2,1)}, u32[]{:S(2)}, u32[]{:S(2)}) collective-permute-start(bf16[2,1,256,16,64]{2,4,3,0,1:T(8,128)(2,1)} %collective-permute-done), channel_id=1, source_target_pairs={{0,16},{16,32},{32,48},{48,64},{64,80},{80,96},{96,112},{112,128},... | collective-permute-start | bytes 3145736 | tf_op jit(solution)/shard_map/ppermute | solution.py:17
  58.9 16.5 %collective-permute-start.3 = (bf16[2,1,256,16,64]{2,4,3,1,0:T(8,128)(2,1)}, bf16[2,1,256,16,64]{2,4,3,1,0:T(8,128)(2,1)S(1)}, u32[]{:S(2)}, u32[]{:S(2)}) collective-permute-start(bf16[2,1,256,16,64]{2,4,3,1,0:T(8,128)(2,1)} %collective-permute-done.2), channel_id=1, source_target_pairs={{0,240},{16,0},{32,16},{48,32},{64,48},{80,64},{96,80},{112,96},{1... | collective-permute-start | bytes 3145736 | tf_op jit(solution)/shard_map/ppermute | solution.py:17
  58.9 14.9 %copy-start.2 = (bf16[1,1,256,16,32]{2,4,3,1,0:T(8,128)(2,1)S(1)}, bf16[1,1,256,16,32]{2,4,3,1,0:T(8,128)(2,1)}, u32[]{:S(2)}) copy-start(bf16[1,1,256,16,32]{2,4,3,1,0:T(8,128)(2,1)} %copy-done.1) | copy-start | bytes 786436
  75.4 2.8 copy-start.3
  171.2 2.8 copy-start.4
  174.0 48.7 %collective-permute-start.4 = (f32[2,1,256,16,64]{2,4,3,0,1:T(8,128)S(1)}, f32[2,1,256,16,64]{2,4,3,0,1:T(8,128)S(1)}, u32[]{:S(2)}, u32[]{:S(2)}) collective-permute-start(f32[2,1,256,16,64]{2,4,3,0,1:T(8,128)S(1)} %get-tuple-element.242), channel_id=1, source_target_pairs={{0,240},{16,0},{32,16},{48,32},{64,48},{80,64},{96,80},{112,96},{1... | collective-permute-start | bytes 6291464 | tf_op jit(solution)/shard_map/ppermute | solution.py:17
  174.1 58.2 %collective-permute-start.6 = (f32[2,1,256,16,64]{2,4,3,0,1:T(8,128)S(1)}, f32[2,1,256,16,64]{2,4,3,0,1:T(8,128)S(1)}, u32[]{:S(2)}, u32[]{:S(2)}) collective-permute-start(f32[2,1,256,16,64]{2,4,3,0,1:T(8,128)S(1)} %get-tuple-element.243), channel_id=1, source_target_pairs={{0,16},{16,32},{32,48},{48,64},{64,80},{80,96},{96,112},{112,128},... | collective-permute-start | bytes 6291464 | tf_op jit(solution)/shard_map/ppermute | solution.py:17
  224.7 48.2 %collective-permute-start.5 = (f32[2,1,256,16,64]{2,4,3,0,1:T(8,128)S(1)}, f32[2,1,256,16,64]{2,4,3,0,1:T(8,128)S(1)}, u32[]{:S(2)}, u32[]{:S(2)}) collective-permute-start(f32[2,1,256,16,64]{2,4,3,0,1:T(8,128)S(1)} %fusion.35), channel_id=1, source_target_pairs={{0,240},{16,0},{32,16},{48,32},{64,48},{80,64},{96,80},{112,96},{1... | collective-permute-start | bytes 6291464 | tf_op jit(solution)/shard_map/ppermute | solution.py:17
  234.3 38.6 %collective-permute-start.7 = (f32[2,1,256,16,64]{2,4,3,1,0:T(8,128)S(1)}, f32[2,1,256,16,64]{2,4,3,1,0:T(8,128)S(1)}, u32[]{:S(2)}, u32[]{:S(2)}) collective-permute-start(f32[2,1,256,16,64]{2,4,3,1,0:T(8,128)S(1)} %fusion.34), channel_id=1, source_target_pairs={{0,16},{16,32},{32,48},{48,64},{64,80},{80,96},{96,112},{112,128},... | collective-permute-start | bytes 6291464 | tf_op jit(solution)/shard_map/ppermute | solution.py:17
  281.9 146.0 %copy-start.5 = (bf16[16,1,256,64]{2,3,1,0:T(8,128)(2,1)S(1)}, bf16[16,1,256,64]{2,3,1,0:T(8,128)(2,1)}, u32[]{:S(2)}) copy-start(bf16[16,1,256,64]{2,3,1,0:T(8,128)(2,1)} %copy-done.4) | copy-start | bytes 1572868
  281.9 347.3 %reduce-scatter.7.cloned.1.call-start = ((), (), s32[]{:S(2)}) async-start(), calls=%async_computation.3 | async-start | bytes 1114112
Sparse Core Ops, SparseCore 0:
  282.0 143.3 reduce-scatter.4
  429.8 199.3 reduce-scatter.6
where the time goes:
time: 643 us; the launch traced here: 636 us
  waiting for transfers between devices  472 us (73%)
  matrix products  56.2 us (9%)
  local copies, waits for them, and re-layouts  52.6 us (8%)
  other arithmetic  29.7 us (5%)
  between operations  14.3 us (2%)
  starting transfers between devices  9.99 us (2%)
    unnamed x3, waiting for transfers between devices  195 us
    reduce_scatter x1, waiting for transfers between devices, per_device(): lax.psum_scatter(weight_term, 'lon', scatter_dimension=1, tiled=True)  143 us
    ppermute x8, waiting for transfers between devices, from_behind(): lax.ppermute(value, axis, [(i, (i + by) % size) for i in range(size)])  134 us
    squeeze x32, local copies, waits for them, and re-layouts, per_device(): lax.map(forward_head, (query_heads, head_major(stacked)))  32 us
    dot_general x32, matrix products, block_scores(): jnp.einsum('mch,emih->mcei', single_query, single_key, preferred_element_...  15 us
    dynamic_update_slice x16, other arithmetic, per_device(): lax.map(backward_head, (query_heads, head_major(stacked_back), out_heads,...  14.3 us
  transfers between devices with their start and end apart: 10, of which 8 were waited for; matrix products, arithmetic and copies ran while one was open for 2% of the time, Pallas kernels for 0%

commit v1 on v0

v1 whole, which is shorter than its diff:
```python
import functools

import jax
import jax.numpy as jnp
from jax import lax
from jax.experimental import pallas as pl
from jax.experimental.pallas import tpu as pltpu
from jax.sharding import PartitionSpec as P

HEADS = 16
W_MAX = 2
INTERP = 0.25
BASE = 10000.0
FAR = 1e30
LOG2E = 1.4426950408889634
BF = jnp.bfloat16
F32 = jnp.float32
MESH = pl.DeviceIdType.MESH
N_LON = 16
ROWS = 256
GROUPS = 4
SLOTS = 5


def dot(a, b):
    return lax.dot_general(a, b, (((1,), (0,)), ((), ())), preferred_element_type=F32)


def dot_t(a, b):
    return lax.dot_general(a, b, (((1,), (1,)), ((), ())), preferred_element_type=F32)


def lanes(shape):
    return lax.broadcasted_iota(jnp.int32, shape, len(shape) - 1)


def perm_matrix():
    source = lax.broadcasted_iota(jnp.int32, (256, 256), 0)
    column = lax.broadcasted_iota(jnp.int32, (256, 256), 1)
    wanted = (column // 32 % 4) * 64 + (column // 128) * 32 + column % 32
    return jnp.where(source == wanted, 1.0, 0.0).astype(BF)


def turn(value, cosine, sine):
    a, c = value[:, :128], value[:, 128:]
    return jnp.concatenate([a * cosine - c * sine, a * sine + c * cosine], axis=1)


def turn_back(value, cosine, sine):
    a, c = value[:, :128], value[:, 128:]
    return jnp.concatenate([a * cosine + c * sine, c * cosine - a * sine], axis=1)


def query_kernel(bias_ref, x_ref, wq_ref, wk_ref, wv_ref, cos_ref, sin_ref, up_ref,
                 out_ref, dq_ref, q_ref, k_ref, v_ref, stats_ref, kbuf, vbuf, stats):
    group = pl.program_id(0)
    perm = perm_matrix()
    wq = dot(wq_ref[...], perm).astype(BF)
    wk = dot(wk_ref[...], perm).astype(BF)
    wv = wv_ref[...]
    for slot in range(SLOTS):
        x = x_ref[slot]
        cosine, sine = cos_ref[slot], sin_ref[slot]
        rows = slice(slot * ROWS, (slot + 1) * ROWS)
        q_ref[rows] = (turn(dot(x, wq), cosine, sine).astype(BF).astype(F32) * 0.125).astype(BF)
        kbuf[rows] = turn(dot(x, wk), cosine, sine).astype(BF)
        vbuf[rows] = dot(x, wv).astype(BF)
    k_ref[...] = kbuf[:ROWS]
    v_ref[...] = vbuf[:ROWS]
    lane = lanes((ROWS, 256))
    lane_pair = lane // 32 % 4
    lane_flat = lane // 64
    stat_lane = lanes((ROWS, 128))
    query = q_ref[:ROWS]
    up = up_ref[...]
    zero = jnp.zeros((), BF)
    out = jnp.zeros((ROWS, 256), F32)
    dquery = jnp.zeros((ROWS, 256), F32)

    @pl.when(group == 0)
    def _():
        stats[...] = jnp.zeros_like(stats)

    for head in range(4):
        own_pair = lane_pair == head
        own_flat = lane_flat == head
        scores = dot_t(jnp.where(own_pair, query, zero), kbuf[...]) * LOG2E
        row_max = None
        for slot in range(SLOTS):
            one = jnp.max(scores[:, slot * ROWS:(slot + 1) * ROWS], axis=1, keepdims=True) - bias_ref[0, slot]
            row_max = one if row_max is None else jnp.maximum(row_max, one)
        parts = []
        total = None
        for slot in range(SLOTS):
            one = jnp.exp2(scores[:, slot * ROWS:(slot + 1) * ROWS] - (row_max + bias_ref[0, slot]))
            part_sum = jnp.sum(one, axis=1, keepdims=True)
            total = part_sum if total is None else total + part_sum
            parts.append(one)
        weights = jnp.concatenate(parts, axis=1)
        inverse = 1.0 / total
        attended = dot(weights.astype(BF), vbuf[...]) * inverse
        attended = attended.astype(BF).astype(F32)
        out = jnp.where(own_flat, attended, out)
        up_own = jnp.where(own_flat, up, zero)
        delta = jnp.sum(up_own.astype(F32) * attended, axis=1, keepdims=True)
        dprobs = dot_t(up_own, vbuf[...])
        dscores = (weights * (dprobs - delta)).astype(BF)
        dquery = jnp.where(own_pair, dot(dscores, kbuf[...]) * (inverse * 0.125), dquery)
        index = group * 4 + head
        now = stats[...]
        now = jnp.where(stat_lane == index, row_max + jnp.log2(total), now)
        stats[...] = jnp.where(stat_lane == index + HEADS, delta, now)
    out_ref[...] = out.astype(BF)
    dquery = turn_back(dquery, cos_ref[0], sin_ref[0]).astype(BF)
    dq_ref[...] = dot_t(dquery, perm).astype(BF)

    @pl.when(group == GROUPS - 1)
    def _():
        stats_ref[...] = stats[...].T[:2 * HEADS]


def key_kernel(lse_ref, delta_ref, q_ref, up_ref, k_ref, v_ref, cos_ref, sin_ref, dk_ref, dv_ref):
    group = pl.program_id(0)
    perm = perm_matrix()
    lane = lanes((ROWS, 256))
    lane_pair = lane // 32 % 4
    lane_flat = lane // 64
    zero = jnp.zeros((), BF)
    key, value = k_ref[...], v_ref[...]
    dkey = jnp.zeros((ROWS, 256), F32)
    dvalue = jnp.zeros((ROWS, 256), F32)
    for head in range(4):
        own_pair = lane_pair == head
        own_flat = lane_flat == head
        lse = lse_ref[pl.ds(group * 4 + head, 1), :]
        delta = delta_ref[pl.ds(group * 4 + head, 1), :]
        scores = dot_t(jnp.where(own_pair, key, zero), q_ref[...]) * LOG2E
        probs = jnp.exp2(scores - lse)
        dprobs = dot_t(jnp.where(own_flat, value, zero), up_ref[...])
        dscores = (probs * (dprobs - delta)).astype(BF)
        dvalue = jnp.where(own_flat, dot(probs.astype(BF), up_ref[...]), dvalue)
        dkey = jnp.where(own_pair, dot(dscores, q_ref[...]), dkey)
    dkey = turn_back(dkey, cos_ref[...], sin_ref[...]).astype(BF)
    dk_ref[...] = dot_t(dkey, perm).astype(BF)
    dv_ref[...] = dvalue.astype(BF)


def run_query(bias, x5, w, cos5, sin5, up):
    full = lambda *shape: pl.BlockSpec(shape, lambda g: (0,) * len(shape))
    col = lambda rows: pl.BlockSpec((rows, 256), lambda g: (0, g))
    bf = lambda rows: jax.ShapeDtypeStruct((rows, 1024), BF)
    return pl.pallas_call(
        query_kernel,
        grid=(GROUPS,),
        in_specs=[
            pl.BlockSpec(memory_space=pltpu.SMEM),
            full(SLOTS, ROWS, 1024),
            pl.BlockSpec((1024, 256), lambda g: (0, g)),
            pl.BlockSpec((1024, 256), lambda g: (0, g + 4)),
            pl.BlockSpec((1024, 256), lambda g: (0, g + 8)),
            full(SLOTS, ROWS, 128),
            full(SLOTS, ROWS, 128),
            col(ROWS),
        ],
        out_specs=[col(ROWS), col(ROWS), col(SLOTS * ROWS), col(ROWS), col(ROWS), full(2 * HEADS, ROWS)],
        out_shape=[bf(ROWS), bf(ROWS), bf(SLOTS * ROWS), bf(ROWS), bf(ROWS),
                   jax.ShapeDtypeStruct((2 * HEADS, ROWS), F32)],
        scratch_shapes=[pltpu.VMEM((SLOTS * ROWS, 256), BF), pltpu.VMEM((SLOTS * ROWS, 256), BF),
                        pltpu.VMEM((ROWS, 128), F32)],
        compiler_params=pltpu.CompilerParams(vmem_limit_bytes=60 * 2**20),
        cost_estimate=pl.CostEstimate(flops=30 * 10**9, bytes_accessed=12 * 2**20, transcendentals=5 * 2**20),
        name="query_side",
    )(bias, x5, w, w, w, cos5, sin5, up)


def run_key(lse, delta, q5, up5, k, v, cosine, sine):
    full = lambda *shape: pl.BlockSpec(shape, lambda g: (0,) * len(shape))
    col = lambda rows: pl.BlockSpec((rows, 256), lambda g: (0, g))
    bf = lambda rows: jax.ShapeDtypeStruct((rows, 1024), BF)
    return pl.pallas_call(
        key_kernel,
        grid=(GROUPS,),
        in_specs=[full(HEADS, SLOTS * ROWS), full(HEADS, SLOTS * ROWS), col(SLOTS * ROWS), col(SLOTS * ROWS),
                  col(ROWS), col(ROWS), full(ROWS, 128), full(ROWS, 128)],
        out_specs=[col(ROWS), col(ROWS)],
        out_shape=[bf(ROWS), bf(ROWS)],
        compiler_params=pltpu.CompilerParams(vmem_limit_bytes=60 * 2**20),
        cost_estimate=pl.CostEstimate(flops=12 * 10**9, bytes_accessed=8 * 2**20, transcendentals=5 * 2**20),
        name="key_side",
    )(lse, delta, q5, up5, k, v, cosine, sine)


def weight_kernel(x_ref, d_ref, g_ref):
    g_ref[0] = dot(x_ref[...], d_ref[...]).astype(BF)


def run_weight(x_rows, d_both):
    return pl.pallas_call(
        weight_kernel,
        grid=(8,),
        in_specs=[pl.BlockSpec((512, 512), lambda c: (0, 0)), pl.BlockSpec((512, 384), lambda c: (0, c))],
        out_specs=pl.BlockSpec((1, 512, 384), lambda c: (c, 0, 0)),
        out_shape=jax.ShapeDtypeStruct((8, 512, 384), BF),
        name="weight_partial",
    )(x_rows, d_both)


def reduce_kernel(g_ref, o_ref, in_x, in_y, sum_a, sum_b, in_a, in_b, sum_p, in_z, mine, theirs,
                  send_x, recv_x, send_y, recv_y, send_a, recv_a, send_b, recv_b, send_z, recv_z, send_c, recv_c):
    lon, dates = lax.axis_index("lon"), lax.axis_index("dates")
    x, y_lo, core = lon // 4, lon // 2 % 2, lon % 2
    z, y_hi = dates // 2, dates % 2
    y = y_hi * 2 + y_lo

    def at(px, py, pz, pc):
        return {"lon": px * 4 + py % 2 * 2 + pc, "dates": pz * 2 + py // 2}

    x_peers = [lax.rem(x + step, 4) for step in (1, 2, 3)]
    y_peers = [lax.rem(y + step, 4) for step in (1, 2, 3)]
    z_peers = [lax.rem(z + step, 8) for step in range(1, 8)]
    barrier = pltpu.get_barrier_semaphore()
    peers = [at(p, y, z, core) for p in x_peers] + [at(x, p, z, core) for p in y_peers]
    peers += [at(x, y, p, core) for p in z_peers] + [at(x, y, z, 1 - core)]
    for peer in peers:
        pl.semaphore_signal(barrier, inc=1, device_id=peer, device_id_type=MESH)
    pl.semaphore_wait(barrier, len(peers))

    def send(source, target, send_sem, recv_sem, peer):
        copy = pltpu.make_async_remote_copy(src_ref=source, dst_ref=target, send_sem=send_sem, recv_sem=recv_sem,
                                            device_id=peer, device_id_type=MESH)
        copy.start()
        return copy

    first_a = [send(g_ref.at[p, :, pl.ds(0, 4)], in_x.at[i], send_x.at[i], recv_x.at[i], at(p, y, z, core))
               for i, p in enumerate(x_peers)]
    first_b = [send(g_ref.at[:, p % 2, pl.ds(4, 4), p // 2], in_y.at[i], send_y.at[i], recv_y.at[i], at(x, p, z, core))
               for i, p in enumerate(y_peers)]
    for copy in first_a:
        copy.wait()
    for lo in range(2):
        for hi in range(2):
            total = g_ref[x, lo, 0:4, hi].astype(F32)
            for i in range(3):
                total += in_x[i, lo, :, hi].astype(F32)
            sum_a[hi, lo] = total.astype(BF)
    second_a = [send(sum_a.at[p // 2, p % 2], in_a.at[i], send_a.at[i], recv_a.at[i], at(x, p, z, core))
                for i, p in enumerate(y_peers)]
    for copy in first_b:
        copy.wait()
    for px in range(4):
        total = g_ref[px, y_lo, 4:8, y_hi].astype(F32)
        for i in range(3):
            total += in_y[i, px].astype(F32)
        sum_b[px] = total.astype(BF)
    second_b = [send(sum_b.at[p], in_b.at[i], send_b.at[i], recv_b.at[i], at(p, y, z, core))
                for i, p in enumerate(x_peers)]
    for copy in second_a:
        copy.wait()
    total = sum_a[y_hi, y_lo].astype(F32)
    for i in range(3):
        total += in_a[i].astype(F32)
    sum_p[0:4] = total.astype(BF)
    for copy in second_b:
        copy.wait()
    total = sum_b[x].astype(F32)
    for i in range(3):
        total += in_b[i].astype(F32)
    sum_p[4:8] = total.astype(BF)
    third = [send(sum_p.at[p], in_z.at[i], send_z.at[i], recv_z.at[i], at(x, y, p, core))
             for i, p in enumerate(z_peers)]
    for copy in third:
        copy.wait()
    total = sum_p[z].astype(F32)
    for i in range(7):
        total += in_z[i].astype(F32)
    total = total * (65536.0 ** -0.5)
    mine[0] = total[:, :192]
    mine[1] = total[:, 192:]
    last = send(mine.at[1 - core], theirs, send_c, recv_c, at(x, y, z, 1 - core))
    last.wait()
    own = mine[core]
    other = theirs[...]
    o_ref[pl.ds(pl.multiple_of(core * 32, 32), 32), :] = own
    o_ref[pl.ds(pl.multiple_of(32 - core * 32, 32), 32), :] = other


def run_reduce(partial):
    dma = pltpu.SemaphoreType.DMA
    return pl.pallas_call(
        reduce_kernel,
        in_specs=[pl.BlockSpec(memory_space=pltpu.VMEM)],
        out_specs=pl.BlockSpec(memory_space=pltpu.VMEM),
        out_shape=jax.ShapeDtypeStruct((64, 192), F32),
        scratch_shapes=[
            pltpu.VMEM((3, 2, 4, 2, 32, 384), BF),
            pltpu.VMEM((3, 4, 4, 32, 384), BF),
            pltpu.VMEM((2, 2, 4, 32, 384), BF),
            pltpu.VMEM((4, 4, 32, 384), BF),
            pltpu.VMEM((3, 4, 32, 384), BF),
            pltpu.VMEM((3, 4, 32, 384), BF),
            pltpu.VMEM((8, 32, 384), BF),
            pltpu.VMEM((7, 32, 384), BF),
            pltpu.VMEM((2, 32, 192), F32),
            pltpu.VMEM((32, 192), F32),
            dma((3,)), dma((3,)), dma((3,)), dma((3,)), dma((3,)), dma((3,)), dma((3,)), dma((3,)),
            dma((7,)), dma((7,)), dma, dma,
        ],
        compiler_params=pltpu.CompilerParams(collective_id=0, has_side_effects=True, vmem_limit_bytes=40 * 2**20),
        name="weight_reduce",
    )(partial.reshape(4, 2, 8, 2, 32, 384))


SWAP = [(i, i ^ 1) for i in range(N_LON)]
NEAR = [(i, (i + (1 if i % 2 else -1)) % N_LON) for i in range(N_LON)]
WIDE = [(i, (i + (-2 if i % 2 else 2)) % N_LON) for i in range(N_LON)]


def gather_halo(value):
    partner = lax.ppermute(value, "lon", SWAP)
    near = lax.ppermute(value, "lon", NEAR)
    wide = lax.ppermute(value, "lon", WIDE)
    passed = lax.ppermute(near, "lon", SWAP)
    return [value, partner, near, wide, passed]


def per_device(features, w_qkv, grad_out, positions, block_list):
    x, up = features[0], grad_out[0]
    core = lax.axis_index("lon") % 2
    toward = 1 - 2 * core
    offsets = jnp.stack([jnp.int32(0), toward, -toward, -2 * toward, 2 * toward])
    listed = block_list[0]
    used = jnp.any(listed[None, :] == offsets[:, None], axis=1)
    used_by = jnp.any(listed[None, :] == -offsets[:, None], axis=1)
    bias = jnp.where(used, 0.0, FAR).astype(F32).reshape(1, SLOTS)

    pair_index = jnp.arange(32, dtype=F32)
    frequency = INTERP * BASE ** (-2.0 * pair_index / 64)
    spots = jnp.concatenate(gather_halo(positions), axis=0)
    angles = spots.astype(F32)[..., None] * frequency
    cos5 = jnp.tile(jnp.cos(angles), (1, 1, 4))
    sin5 = jnp.tile(jnp.sin(angles), (1, 1, 4))
    x5 = jnp.stack(gather_halo(x))
    up5 = jnp.concatenate(gather_halo(up), axis=0)
    out, dq, q5, k, v, stats = run_query(bias, x5, w_qkv, cos5, sin5, up)
    stats5 = jnp.stack(gather_halo(stats))
    lse = stats5[:, :HEADS] + jnp.where(used_by, 0.0, FAR)[:, None, None]
    delta = stats5[:, HEADS:]
    lse = jnp.transpose(lse, (1, 0, 2)).reshape(HEADS, SLOTS * ROWS)
    delta = jnp.transpose(delta, (1, 0, 2)).reshape(HEADS, SLOTS * ROWS)
    dk, dv = run_key(lse, delta, q5, up5, k, v, cos5[0], sin5[0])
    dqkv = jnp.concatenate([dq, dk, dv], axis=1)
    d_other = lax.ppermute(dqkv, "lon", SWAP)
    grad_x = lax.dot_general(dqkv, w_qkv, (((1,), (1,)), ((), ())), preferred_element_type=F32).astype(BF)
    tokens = x5[:2].reshape(2 * ROWS, 16, 2, 32)
    x_rows = lax.dynamic_index_in_dim(tokens, core, axis=2, keepdims=False).reshape(2 * ROWS, 512).T
    partial = run_weight(x_rows, jnp.concatenate([dqkv, d_other], axis=0))
    grad_w = run_reduce(partial)
    return (out[None], grad_x[None], grad_w)


def solution(mesh):
    return jax.shard_map(
        per_device,
        mesh=mesh,
        in_specs=(
            P("dates", "lon", None),
            P(),
            P("dates", "lon", None),
            P("dates", "lon"),
            P("dates", None),
        ),
        out_specs=(P("dates", "lon", None), P("dates", "lon", None), P("dates", "lon")),
        check_vma=False,
    )
```

time: 643 us -> 186 us (0.29)
  waiting for transfers between devices: 472 us -> 25.3 us
  Pallas kernels: 0 us -> 100 us
  matrix products: 56.2 us -> 5.89 us
  other arithmetic: 29.7 us -> 6.05 us
  local copies, waits for them, and re-layouts: 52.6 us -> 30.1 us
  between operations: 14.3 us -> 0.78 us
    unnamed x3 -> x0, waiting for transfers between devices: 195 us -> none
    reduce_scatter x1 -> x0, waiting for transfers between devices: 143 us -> none  [per_device(): lax.psum_scatter(weight_term, 'lon', scatter_dimension=1, tiled=True)]
    ppermute x8 -> x17, waiting for transfers between devices: 134 us -> 25.3 us  [the longest x4 23.9 us: gather_halo(): near = lax.ppermute(value, 'lon', NEAR)]
    pallas_call x0 -> x4, Pallas kernels: none -> 100 us  [the longest x1 42.6 us: run_reduce(): pl.pallas_call(reduce_kernel, in_specs=[pl.BlockSpec(memory_space=pltpu.V...]
    dot_general x115 -> x1, matrix products: 56.2 us -> 5.89 us  [per_device(): lax.dot_general(dqkv, w_qkv, (((1,), (1,)), ((), ())), preferred_element_...]
    squeeze x34 -> x0, local copies, waits for them, and re-layouts: 34.9 us -> none  [the longest x32 32 us: per_device(): lax.map(forward_head, (query_heads, head_major(stacked)))]
    dynamic_update_slice x16 -> x0, other arithmetic: 14.3 us -> none  [per_device(): lax.map(backward_head, (query_heads, head_major(stacked_back), out_heads,...]
    unnamed x24 -> x19, local copies, waits for them, and re-layouts: 9.27 us -> 18 us
  transfers between devices with their start and end apart: 10 -> 17, of which waited for: 8 -> 4; matrix products, arithmetic and copies ran while one was open for 2% -> 17% of each run, Pallas kernels for 0% -> 19%
where the time goes in v1:
time: 186 us; the launch traced here: 182 us
  Pallas kernels  100 us (54%)
  local copies, waits for them, and re-layouts  30.1 us (16%)
  waiting for transfers between devices  25.3 us (14%)
  starting transfers between devices  14.1 us (8%)
  other arithmetic  6.05 us (3%)
  matrix products  5.89 us (3%)
    pallas_call x1, Pallas kernels, run_reduce(): pl.pallas_call(reduce_kernel, in_specs=[pl.BlockSpec(memory_space=pltpu.V...  42.6 us
    pallas_call x1, Pallas kernels, run_query(): pl.pallas_call(query_kernel, grid=(GROUPS,), in_specs=[pl.BlockSpec(memor...  34.1 us
    ppermute x4, waiting for transfers between devices, gather_halo(): near = lax.ppermute(value, 'lon', NEAR)  23.9 us
    unnamed x19, local copies, waits for them, and re-layouts  18 us
    pallas_call x1, Pallas kernels, run_key(): pl.pallas_call(key_kernel, grid=(GROUPS,), in_specs=[full(HEADS, SLOTS *...  15.6 us
    pallas_call x1, Pallas kernels, run_weight(): pl.pallas_call(weight_kernel, grid=(8,), in_specs=[pl.BlockSpec((512, 512...  7.84 us
    dot_general x1, matrix products, per_device(): lax.dot_general(dqkv, w_qkv, (((1,), (1,)), ((), ())), preferred_element_...  5.89 us
    ppermute x4, starting transfers between devices, gather_halo(): wide = lax.ppermute(value, 'lon', WIDE)  4.28 us
  transfers between devices with their start and end apart: 17, of which 4 were waited for; matrix products, arithmetic and copies ran while one was open for 17% of the time, Pallas kernels for 19%

profile of v1, /device:TPU:7, one launch (start us, length us, event | category | flops | bytes accessed | tf_op | source)
XLA Modules:
  0.0 182.4 jit_solution(16908131360078225434)
XLA Ops:
  0.6 0.8 collective-permute-start
  1.4 1.3 collective-permute-start.1
  3.1 1.0 collective-permute-start.4
  4.1 1.5 collective-permute-start.6
  5.7 0.9 compare_reduce_fusion
  7.1 1.9 %constant_dynamic-update-slice_fusion.11 = bf16[1280,1024]{1,0:T(8,128)(2,1)} fusion(bf16[1,256,1024]{2,1,0:T(8,128)(2,1)} %param.7), kind=kLoop, calls=%fused_computation.24 | loop fusion | bytes 1048576
  9.0 1.9 %constant_dynamic-update-slice_fusion.1 = bf16[5,256,1024]{2,1,0:T(8,128)(2,1)} fusion(bf16[1,256,1024]{2,1,0:T(8,128)(2,1)} %param.5), kind=kLoop, calls=%fused_computation.14 | loop fusion | bytes 1048576
  10.9 5.0 %collective-permute-done.5 = s32[1,256]{1,0:T(1,128)S(1)} collective-permute-done((s32[1,256]{1,0:T(1,128)}, s32[1,256]{1,0:T(1,128)S(1)}, u32[]{:S(2)}, u32[]{:S(2)}) %collective-permute-start.5) | collective-permute-done | bytes 1056 | tf_op jit(solution)/shard_map/ppermute | solution.py:320
  15.9 1.4 collective-permute-start.13
  17.3 0.8 collective-permute-start.12
  18.1 0.8 collective-permute-start.14
  18.9 0.7 concatenate.21
  19.6 0.6 multiply_sine_fusion
  20.5 1.1 copy.18.cos_ref
  21.7 1.2 copy.19.sin_ref
  22.9 0.8 copy.22.cos_ref
  23.7 0.8 copy.23.sin_ref
  24.4 0.7 collective-permute-start.2
  25.1 2.5 %collective-permute-start.3 = (bf16[256,1024]{1,0:T(8,128)(2,1)S(1)}, bf16[256,1024]{1,0:T(8,128)(2,1)S(1)}, u32[]{:S(2)}, u32[]{:S(2)}) collective-permute-start(bf16[256,1024]{1,0:T(8,128)(2,1)S(1)} %collective-permute-done.1), channel_id=1, source_target_pairs={{0,16},{16,0},{32,48},{48,32},{64,80},{80,64},{96,112},{112,96},{1... | collective-permute-start | bytes 1572872 | tf_op jit(solution)/shard_map/ppermute | solution.py:322
  27.6 18.9 %collective-permute-done.13 = bf16[256,1024]{1,0:T(8,128)(2,1)S(1)} collective-permute-done((bf16[256,1024]{1,0:T(8,128)(2,1)}, bf16[256,1024]{1,0:T(8,128)(2,1)S(1)}, u32[]{:S(2)}, u32[]{:S(2)}) %collective-permute-start.13) | collective-permute-done | bytes 524320 | tf_op jit(solution)/shard_map/ppermute | solution.py:320
  46.5 0.8 constant_dynamic-update-slice_fusion
  47.3 1.9 %constant_dynamic-update-slice_fusion.10 = bf16[1280,1024]{1,0:T(8,128)(2,1)} fusion(bf16[1280,1024]{1,0:T(8,128)(2,1)} %constant_dynamic-update-slice_fusion.11, bf16[256,1024]{1,0:T(8,128)(2,1)} %collective-permute-done.12), kind=kLoop, calls=%fused_computation.23 | loop fusion | bytes 1048576
  49.2 0.8 constant_dynamic-update-slice_fusion.9
  50.1 1.9 %constant_dynamic-update-slice_fusion.8 = bf16[1280,1024]{1,0:T(8,128)(2,1)} fusion(bf16[1280,1024]{1,0:T(8,128)(2,1)} %constant_dynamic-update-slice_fusion.9, bf16[256,1024]{1,0:T(8,128)(2,1)} %collective-permute-done.14), kind=kLoop, calls=%fused_computation.21 | loop fusion | bytes 1048576
  51.9 0.8 bitcast_dynamic-update-slice_fusion.2
  52.9 0.8 bitcast_dynamic-update-slice_fusion.1
  53.8 0.8 bitcast_dynamic-update-slice_fusion.x_ref
  54.6 34.1 %query_side.1 = (bf16[256,1024]{1,0:T(8,128)(2,1)}, bf16[256,1024]{1,0:T(8,128)(2,1)}, bf16[1280,1024]{1,0:T(8,128)(2,1)}, bf16[256,1024]{1,0:T(8,128)(2,1)}, bf...) custom-call(f32[1,5]{1,0:T(1,128)} %select_bitcast_fusion.bias_ref, ...), custom_call_target="tpu_custom_call" | custom-call | flops 30000001024 | bytes 12582912 | tf_op jit(solution)/shard_map/query_side/pallas_call | solution.py:152
  89.1 1.1 collective-permute-start.9
  90.2 1.4 collective-permute-start.10
  91.6 1.9 %constant_dynamic-update-slice_fusion.14 = bf16[256,3072]{1,0:T(8,128)(2,1)} fusion(bf16[256,1024]{1,0:T(8,128)(2,1)} %get-tuple-element.12), kind=kLoop, calls=%fused_computation.27 | loop fusion | bytes 1048576
  93.5 0.8 constant_dynamic-update-slice_fusion.6
  94.3 0.8 constant_dynamic-update-slice_fusion.7.up_ref
  95.2 1.1 collective-permute-done.11
  96.4 0.6 copy.25
  97.0 0.6 copy.26
  97.7 15.6 %key_side.1 = (bf16[256,1024]{1,0:T(8,128)(2,1)}, bf16[256,1024]{1,0:T(8,128)(2,1)}) custom-call(f32[16,1280]{1,0:T(8,128)} %bitcast.69, f32[16,1280]{1,0:T(8,128)} %bitcast.70, bf16[1280,1024]{1,0:T(8,128)(2,1)} %get-tuple-element.14.q_ref, bf16[1280,1024]{1,0:T(8,128)(2,1)} %constant_dynamic-update-slice_fusion.7.up_ref, ...), custom_call_target="tpu_custom_call" | custom-call | flops 12000000000 | bytes 8388608 | tf_op jit(solution)/shard_map/key_side/pallas_call | solution.py:180
  113.2 1.9 %constant_dynamic-update-slice_fusion.13 = bf16[256,3072]{1,0:T(8,128)(2,1)} fusion(bf16[256,3072]{1,0:T(8,128)(2,1)} %constant_dynamic-update-slice_fusion.14, bf16[256,1024]{1,0:T(8,128)(2,1)} %get-tuple-element.17), kind=kLoop, calls=%fused_computation.26 | loop fusion | bytes 1048576
  115.1 1.9 %constant_dynamic-update-slice_fusion.12 = bf16[256,3072]{1,0:T(8,128)(2,1)} fusion(bf16[256,3072]{1,0:T(8,128)(2,1)} %constant_dynamic-update-slice_fusion.13, bf16[256,1024]{1,0:T(8,128)(2,1)} %get-tuple-element.18), kind=kLoop, calls=%fused_computation.25 | loop fusion | bytes 1048576 | tf_op jit(solution)/shard_map/concatenate | solution.py:351
  117.3 0.9 copy.24
  118.2 0.7 reshape.148
  118.9 0.8 constant_dynamic-slice_fusion
  119.8 5.9 %fusion = bf16[1,256,1024]{2,1,0:T(8,128)(2,1)} fusion(bf16[256,3072]{1,0:T(8,128)(2,1)} %constant_dynamic-update-slice_fusion.12, bf16[1024,3072]{1,0:T(8,128)(2,1)} %wv_ref.1), kind=kOutput, calls=%fused_computation.2 | convolution fusion | flops 1610874880 | bytes 8388608 | tf_op jit(solution)/shard_map/dot_general | solution.py:353
  125.7 3.7 %pad_maximum_fusion.d_ref = bf16[512,3072]{1,0:T(8,128)(2,1)} fusion(bf16[256,3072]{1,0:T(8,128)(2,1)} %collective-permute-done.16, bf16[256,3072]{1,0:T(8,128)(2,1)} %constant_dynamic-update-slice_fusion.12), kind=kLoop, calls=%fused_computation | loop fusion | flops 6291456 | bytes 6291456 | tf_op jit(solution)/shard_map/concatenate | solution.py:356
  129.4 7.8 %weight_partial.1 = bf16[8,512,384]{2,1,0:T(8,128)(2,1)} custom-call(bf16[512,512]{1,0:T(8,128)(2,1)} %bitcast.62, bf16[512,3072]{1,0:T(8,128)(2,1)} %pad_maximum_fusion.d_ref), custom_call_target="tpu_custom_call" | custom-call | tf_op jit(solution)/shard_map/weight_partial/pallas_call | solution.py:198
  137.2 1.9 %copy-done = bf16[8,512,384]{2,1,0:T(8,128)(2,1)S(1)} copy-done((bf16[8,512,384]{2,1,0:T(8,128)(2,1)S(1)}, bf16[8,512,384]{2,1,0:T(8,128)(2,1)}, u32[]{:S(2)}) %copy-start) | copy-done | bytes 3145752
  139.1 42.6 %weight_reduce.1 = f32[64,192]{1,0:T(8,128)S(1)} custom-call(bf16[4,2,8,2,32,384]{5,4,3,2,1,0:T(8,128)(2,1)S(1)} %bitcast.55), custom_call_target="tpu_custom_call" | custom-call | tf_op jit(solution)/shard_map/weight_reduce/pallas_call | solution.py:289
  181.8 0.6 copy.42
  (41 shorter events, 2.4 us)
Async XLA Ops:
  0.6 23.8 %collective-permute-start = (bf16[256,1024]{1,0:T(8,128)(2,1)}, bf16[256,1024]{1,0:T(8,128)(2,1)S(1)}, u32[]{:S(2)}, u32[]{:S(2)}) collective-permute-start(bf16[256,1024]{1,0:T(8,128)(2,1)} %bitcast.58), channel_id=1, source_target_pairs={{0,16},{16,0},{32,48},{48,32},{64,80},{80,64},{96,112},{112,96},{1... | collective-permute-start | bytes 1572872 | tf_op jit(solution)/shard_map/ppermute | solution.py:319
  1.4 23.7 %collective-permute-start.1 = (bf16[256,1024]{1,0:T(8,128)(2,1)}, bf16[256,1024]{1,0:T(8,128)(2,1)S(1)}, u32[]{:S(2)}, u32[]{:S(2)}) collective-permute-start(bf16[256,1024]{1,0:T(8,128)(2,1)} %bitcast.59), channel_id=1, source_target_pairs={{0,240},{16,32},{32,16},{48,64},{64,48},{80,96},{96,80},{112,128},... | collective-permute-start | bytes 1572872 | tf_op jit(solution)/shard_map/ppermute | solution.py:320
  2.7 13.2 %collective-permute-start.5 = (s32[1,256]{1,0:T(1,128)}, s32[1,256]{1,0:T(1,128)S(1)}, u32[]{:S(2)}, u32[]{:S(2)}) collective-permute-start(s32[1,256]{1,0:T(1,128)} %param.8), channel_id=1, source_target_pairs={{0,240},{16,32},{32,16},{48,64},{64,48},{80,96},{96,80},{112,128},... | collective-permute-start | bytes 3080 | tf_op jit(solution)/shard_map/ppermute | solution.py:320
  3.1 12.8 %collective-permute-start.4 = (s32[1,256]{1,0:T(1,128)}, s32[1,256]{1,0:T(1,128)S(1)}, u32[]{:S(2)}, u32[]{:S(2)}) collective-permute-start(s32[1,256]{1,0:T(1,128)} %param.8), channel_id=1, source_target_pairs={{0,16},{16,0},{32,48},{48,32},{64,80},{80,64},{96,112},{112,96},{1... | collective-permute-start | bytes 3080 | tf_op jit(solution)/shard_map/ppermute | solution.py:319
  4.1 13.2 %collective-permute-start.6 = (s32[1,256]{1,0:T(1,128)}, s32[1,256]{1,0:T(1,128)S(1)}, u32[]{:S(2)}, u32[]{:S(2)}) collective-permute-start(s32[1,256]{1,0:T(1,128)} %param.8), channel_id=1, source_target_pairs={{0,32},{16,240},{32,64},{48,16},{64,96},{80,48},{96,128},{112,80},... | collective-permute-start | bytes 3080 | tf_op jit(solution)/shard_map/ppermute | solution.py:321
  15.9 2.2 %collective-permute-start.7 = (s32[1,256]{1,0:T(1,128)S(1)}, s32[1,256]{1,0:T(1,128)S(1)}, u32[]{:S(2)}, u32[]{:S(2)}) collective-permute-start(s32[1,256]{1,0:T(1,128)S(1)} %collective-permute-done.5), channel_id=1, source_target_pairs={{0,16},{16,0},{32,48},{48,32},{64,80},{80,64},{96,112},{112,96},{1... | collective-permute-start | bytes 3080 | tf_op jit(solution)/shard_map/ppermute | solution.py:322
  15.9 30.6 %collective-permute-start.13 = (bf16[256,1024]{1,0:T(8,128)(2,1)}, bf16[256,1024]{1,0:T(8,128)(2,1)S(1)}, u32[]{:S(2)}, u32[]{:S(2)}) collective-permute-start(bf16[256,1024]{1,0:T(8,128)(2,1)} %bitcast.65), channel_id=1, source_target_pairs={{0,240},{16,32},{32,16},{48,64},{64,48},{80,96},{96,80},{112,128},... | collective-permute-start | bytes 1572872 | tf_op jit(solution)/shard_map/ppermute | solution.py:320
  17.3 30.0 %collective-permute-start.12 = (bf16[256,1024]{1,0:T(8,128)(2,1)}, bf16[256,1024]{1,0:T(8,128)(2,1)}, u32[]{:S(2)}, u32[]{:S(2)}) collective-permute-start(bf16[256,1024]{1,0:T(8,128)(2,1)} %bitcast.66), channel_id=1, source_target_pairs={{0,16},{16,0},{32,48},{48,32},{64,80},{80,64},{96,112},{112,96},{1... | collective-permute-start | bytes 1572872 | tf_op jit(solution)/shard_map/ppermute | solution.py:319
  18.1 32.0 %collective-permute-start.14 = (bf16[256,1024]{1,0:T(8,128)(2,1)}, bf16[256,1024]{1,0:T(8,128)(2,1)}, u32[]{:S(2)}, u32[]{:S(2)}) collective-permute-start(bf16[256,1024]{1,0:T(8,128)(2,1)} %bitcast.67), channel_id=1, source_target_pairs={{0,32},{16,240},{32,64},{48,16},{64,96},{80,48},{96,128},{112,80},... | collective-permute-start | bytes 1572872 | tf_op jit(solution)/shard_map/ppermute | solution.py:321
  20.3 4.1 %copy-start.1 = (bf16[1,256,1024]{2,1,0:T(8,128)(2,1)S(1)}, bf16[1,256,1024]{2,1,0:T(8,128)(2,1)}, u32[]{:S(2)}) copy-start(bf16[1,256,1024]{2,1,0:T(8,128)(2,1)} %param.5) | copy-start | bytes 1572868
  24.4 28.5 %collective-permute-start.2 = (bf16[256,1024]{1,0:T(8,128)(2,1)S(1)}, bf16[256,1024]{1,0:T(8,128)(2,1)S(1)}, u32[]{:S(2)}, u32[]{:S(2)}) collective-permute-start(bf16[256,1024]{1,0:T(8,128)(2,1)S(1)} %bitcast.60), channel_id=1, source_target_pairs={{0,32},{16,240},{32,64},{48,16},{64,96},{80,48},{96,128},{112,80},... | collective-permute-start | bytes 1572872 | tf_op jit(solution)/shard_map/ppermute | solution.py:321
  25.1 28.7 %collective-permute-start.3 = (bf16[256,1024]{1,0:T(8,128)(2,1)S(1)}, bf16[256,1024]{1,0:T(8,128)(2,1)S(1)}, u32[]{:S(2)}, u32[]{:S(2)}) collective-permute-start(bf16[256,1024]{1,0:T(8,128)(2,1)S(1)} %collective-permute-done.1), channel_id=1, source_target_pairs={{0,16},{16,0},{32,48},{48,32},{64,80},{80,64},{96,112},{112,96},{1... | collective-permute-start | bytes 1572872 | tf_op jit(solution)/shard_map/ppermute | solution.py:322
  46.5 47.8 %collective-permute-start.15 = (bf16[256,1024]{1,0:T(8,128)(2,1)S(1)}, bf16[256,1024]{1,0:T(8,128)(2,1)S(1)}, u32[]{:S(2)}, u32[]{:S(2)}) collective-permute-start(bf16[256,1024]{1,0:T(8,128)(2,1)S(1)} %collective-permute-done.13), channel_id=1, source_target_pairs={{0,16},{16,0},{32,48},{48,32},{64,80},{80,64},{96,112},{112,96},{1... | collective-permute-start | bytes 1572872 | tf_op jit(solution)/shard_map/ppermute | solution.py:322
  88.7 6.4 %collective-permute-start.8 = (f32[32,256]{1,0:T(8,128)}, f32[32,256]{1,0:T(8,128)S(1)}, u32[]{:S(2)}, u32[]{:S(2)}) collective-permute-start(f32[32,256]{1,0:T(8,128)} %get-tuple-element.13), channel_id=1, source_target_pairs={{0,16},{16,0},{32,48},{48,32},{64,80},{80,64},{96,112},{112,96},{1... | collective-permute-start | bytes 98312 | tf_op jit(solution)/shard_map/ppermute | solution.py:319
  89.1 6.0 %collective-permute-start.9 = (f32[32,256]{1,0:T(8,128)}, f32[32,256]{1,0:T(8,128)S(1)}, u32[]{:S(2)}, u32[]{:S(2)}) collective-permute-start(f32[32,256]{1,0:T(8,128)} %get-tuple-element.13), channel_id=1, source_target_pairs={{0,240},{16,32},{32,16},{48,64},{64,48},{80,96},{96,80},{112,128},... | collective-permute-start | bytes 98312 | tf_op jit(solution)/shard_map/ppermute | solution.py:320
  90.2 5.0 %collective-permute-start.10 = (f32[32,256]{1,0:T(8,128)}, f32[32,256]{1,0:T(8,128)S(1)}, u32[]{:S(2)}, u32[]{:S(2)}) collective-permute-start(f32[32,256]{1,0:T(8,128)} %get-tuple-element.13), channel_id=1, source_target_pairs={{0,32},{16,240},{32,64},{48,16},{64,96},{80,48},{96,128},{112,80},... | collective-permute-start | bytes 98312 | tf_op jit(solution)/shard_map/ppermute | solution.py:321
  95.1 1.2 collective-permute-start.11
  117.0 8.6 %collective-permute-start.16 = (bf16[256,3072]{1,0:T(8,128)(2,1)}, bf16[256,3072]{1,0:T(8,128)(2,1)}, u32[]{:S(2)}, u32[]{:S(2)}) collective-permute-start(bf16[256,3072]{1,0:T(8,128)(2,1)} %constant_dynamic-update-slice_fusion.12), channel_id=1, source_target_pairs={{0,16},{16,0},{32,48},{48,32},{64,80},{80,64},{96,112},{112,96},{1... | collective-permute-start | bytes 4718600 | tf_op jit(solution)/shard_map/ppermute | solution.py:352
  137.2 1.9 %copy-start = (bf16[8,512,384]{2,1,0:T(8,128)(2,1)S(1)}, bf16[8,512,384]{2,1,0:T(8,128)(2,1)}, u32[]{:S(2)}) copy-start(bf16[8,512,384]{2,1,0:T(8,128)(2,1)} %weight_partial.1) | copy-start | bytes 9437188

commit v2 on v1

--- a/solution.py
+++ b/solution.py
@@ -51,76 +51,186 @@
     return jnp.concatenate([a * cosine + c * sine, c * cosine - a * sine], axis=1)
 
 
-def query_kernel(bias_ref, x_ref, wq_ref, wk_ref, wv_ref, cos_ref, sin_ref, up_ref,
-                 out_ref, dq_ref, q_ref, k_ref, v_ref, stats_ref, kbuf, vbuf, stats):
-    group = pl.program_id(0)
+def query_kernel(bias_ref, x_hbm, w_hbm, up_hbm, spots_ref, freq_ref,
+                 out_ref, dq_ref, q_ref, k_ref, v_ref, cos_ref, sin_ref, up_out, stats_out,
+                 xs, spots, wbuf, wpair, up, kbuf, vbuf, cos5, sin5,
+                 local, x_send, x_recv, p_send, p_recv, u_send, u_recv, s_send, s_recv):
+    lon = lax.axis_index("lon")
+    core = lax.rem(lon, 2)
+    toward = 1 - 2 * core
+    partner = {"lon": lon + toward}
+    near_lon = lax.rem(lon - toward + N_LON, N_LON)
+    near = {"lon": near_lon}
+    ahead = {"lon": lax.rem(lon + 2 * toward + N_LON, N_LON)}
+    behind = {"lon": lax.rem(lon - 2 * toward + N_LON, N_LON)}
+
+    bring = [pltpu.make_async_copy(x_hbm, xs.at[0], local.at[0]),
+             pltpu.make_async_copy(w_hbm, wbuf, local.at[1]),
+             pltpu.make_async_copy(up_hbm, up, local.at[2])]
+    for copy in bring:
+        copy.start()
+    barrier = pltpu.get_barrier_semaphore()
+    for peer in (partner, near, ahead, behind):
+        pl.semaphore_signal(barrier, inc=1, device_id=peer, device_id_type=MESH)
+    pl.semaphore_wait(barrier, 4)
+
+    def remote(source, target, send_sem, recv_sem, peer):
+        return pltpu.make_async_remote_copy(src_ref=source, dst_ref=target, send_sem=send_sem, recv_sem=recv_sem,
+                                            device_id=peer, device_id_type=MESH)
+
+    routes = ((1, partner), (2, near), (3, ahead))
+    p_copies = {slot: remote(spots_ref, spots.at[slot], p_send.at[slot], p_recv.at[slot], peer) for slot, peer in routes}
+    p_copies[4] = remote(spots.at[2], spots.at[4], p_send.at[4], p_recv.at[4], partner)
+    x_copies = {slot: remote(x_hbm, xs.at[slot], x_send.at[slot], x_recv.at[slot], peer) for slot, peer in routes}
+    x_copies[4] = remote(xs.at[2], xs.at[4], x_send.at[4], x_recv.at[4], partner)
+
+    def block(slot):
+        return pl.ds(slot * ROWS, ROWS)
+
+    u_copies = {slot: remote(up_hbm, up_out.at[block(slot)], u_send.at[slot], u_recv.at[slot], peer)
+                for slot, peer in routes}
+    u_copies[4] = remote(up_out.at[block(2)], up_out.at[block(4)], u_send.at[4], u_recv.at[4], partner)
+    for slot in (2, 1, 3):
+        p_copies[slot].start()
+    x_copies[2].start()
+    x_copies[1].start()
+
     perm = perm_matrix()
-    wq = dot(wq_ref[...], perm).astype(BF)
-    wk = dot(wk_ref[...], perm).astype(BF)
-    wv = wv_ref[...]
-    for slot in range(SLOTS):
-        x = x_ref[slot]
-        cosine, sine = cos_ref[slot], sin_ref[slot]
-        rows = slice(slot * ROWS, (slot + 1) * ROWS)
-        q_ref[rows] = (turn(dot(x, wq), cosine, sine).astype(BF).astype(F32) * 0.125).astype(BF)
-        kbuf[rows] = turn(dot(x, wk), cosine, sine).astype(BF)
-        vbuf[rows] = dot(x, wv).astype(BF)
-    k_ref[...] = kbuf[:ROWS]
-    v_ref[...] = vbuf[:ROWS]
+    bring[0].wait()
+    bring[1].wait()
+
+    @pl.loop(0, 2 * GROUPS)
+    def _(g):
+        cols = pl.ds(pl.multiple_of(g * 256, 256), 256)
+        wpair[:, cols] = dot(wbuf[:, cols], perm).astype(BF)
+
+    def tables(slot, row):
+        spread = jnp.broadcast_to(row, (128, ROWS)).T
+        angle = spread * freq_ref[0:1, :]
+        cos5[slot] = jnp.cos(angle)
+        sin5[slot] = jnp.sin(angle)
+
+    def project(slot):
+        @pl.loop(0, GROUPS)
+        def _(g):
+            def cols(part):
+                return pl.ds(pl.multiple_of(g * 256 + part * 1024, 256), 256)
+
+            x = xs[slot]
+            cosine, sine = cos5[slot], sin5[slot]
+            query = turn(dot(x, wpair[:, cols(0)]), cosine, sine).astype(BF).astype(F32) * 0.125
+            q_ref[block(slot), cols(0)] = query.astype(BF)
+            kbuf[block(slot), cols(0)] = turn(dot(x, wpair[:, cols(1)]), cosine, sine).astype(BF)
+            vbuf[block(slot), cols(0)] = dot(x, wbuf[:, cols(2)]).astype(BF)
+
+    tables(0, spots_ref[0:1, :])
+    project(0)
+    x_copies[2].wait_send()
+    x_copies[3].start()
+    p_copies[1].wait()
+    x_copies[1].wait()
+    tables(1, spots[1, 0:1, :])
+    project(1)
+    p_copies[2].wait()
+    p_copies[4].start()
+    x_copies[2].wait_recv()
+    x_copies[4].start()
+    tables(2, spots[2, 0:1, :])
+    project(2)
+    p_copies[3].wait()
+    p_copies[4].wait()
+    tables(3, spots[3, 0:1, :])
+    tables(4, spots[4, 0:1, :])
+    x_copies[4].wait()
+    project(4)
+    x_copies[3].wait()
+    u_copies[2].start()
+    u_copies[1].start()
+    u_copies[3].start()
+    bring[2].wait()
+    keep_up = pltpu.make_async_copy(up, up_out.at[block(0)], local.at[3])
+    keep_up.start()
+    project(3)
+    k_ref[...] = kbuf[block(0)]
+    v_ref[...] = vbuf[block(0)]
+    cos_ref[...] = cos5[0]
+    sin_ref[...] = sin5[0]
     lane = lanes((ROWS, 256))
     lane_pair = lane // 32 % 4
     lane_flat = lane // 64
     stat_lane = lanes((ROWS, 128))
-    query = q_ref[:ROWS]
-    up = up_ref[...]
     zero = jnp.zeros((), BF)
-    out = jnp.zeros((ROWS, 256), F32)
-    dquery = jnp.zeros((ROWS, 256), F32)
-
-    @pl.when(group == 0)
-    def _():
-        stats[...] = jnp.zeros_like(stats)
-
-    for head in range(4):
-        own_pair = lane_pair == head
-        own_flat = lane_flat == head
-        scores = dot_t(jnp.where(own_pair, query, zero), kbuf[...]) * LOG2E
-        row_max = None
-        for slot in range(SLOTS):
-            one = jnp.max(scores[:, slot * ROWS:(slot + 1) * ROWS], axis=1, keepdims=True) - bias_ref[0, slot]
-            row_max = one if row_max is None else jnp.maximum(row_max, one)
-        parts = []
-        total = None
-        for slot in range(SLOTS):
-            one = jnp.exp2(scores[:, slot * ROWS:(slot + 1) * ROWS] - (row_max + bias_ref[0, slot]))
-            part_sum = jnp.sum(one, axis=1, keepdims=True)
-            total = part_sum if total is None else total + part_sum
-            parts.append(one)
-        weights = jnp.concatenate(parts, axis=1)
-        inverse = 1.0 / total
-        attended = dot(weights.astype(BF), vbuf[...]) * inverse
-        attended = attended.astype(BF).astype(F32)
-        out = jnp.where(own_flat, attended, out)
-        up_own = jnp.where(own_flat, up, zero)
-        delta = jnp.sum(up_own.astype(F32) * attended, axis=1, keepdims=True)
-        dprobs = dot_t(up_own, vbuf[...])
-        dscores = (weights * (dprobs - delta)).astype(BF)
-        dquery = jnp.where(own_pair, dot(dscores, kbuf[...]) * (inverse * 0.125), dquery)
-        index = group * 4 + head
-        now = stats[...]
-        now = jnp.where(stat_lane == index, row_max + jnp.log2(total), now)
-        stats[...] = jnp.where(stat_lane == index + HEADS, delta, now)
-    out_ref[...] = out.astype(BF)
-    dquery = turn_back(dquery, cos_ref[0], sin_ref[0]).astype(BF)
-    dq_ref[...] = dot_t(dquery, perm).astype(BF)
-
-    @pl.when(group == GROUPS - 1)
-    def _():
-        stats_ref[...] = stats[...].T[:2 * HEADS]
-
-
-def key_kernel(lse_ref, delta_ref, q_ref, up_ref, k_ref, v_ref, cos_ref, sin_ref, dk_ref, dv_ref):
-    group = pl.program_id(0)
+
+    def s_copy(g, slot, peer):
+        return remote(stats_out.at[2 if slot == 4 else 0, g], stats_out.at[slot, g],
+                      s_send.at[slot, g], s_recv.at[slot, g], peer)
+
+    @pl.loop(0, GROUPS)
+    def _(g):
+        cols = pl.ds(pl.multiple_of(g * 256, 256), 256)
+        query = q_ref[block(0), cols]
+        keys, values, up_g = kbuf[:, cols], vbuf[:, cols], up[:, cols]
+        out = jnp.zeros((ROWS, 256), F32)
+        dquery = jnp.zeros((ROWS, 256), F32)
+        now = jnp.zeros((ROWS, 128), F32)
+        for head in range(4):
+            own_pair = lane_pair == head
+            own_flat = lane_flat == head
+            scores = dot_t(jnp.where(own_pair, query, zero), keys) * LOG2E
+            row_max = None
+            for slot in range(SLOTS):
+                one = jnp.max(scores[:, slot * ROWS:(slot + 1) * ROWS], axis=1, keepdims=True) - bias_ref[0, slot]
+                row_max = one if row_max is None else jnp.maximum(row_max, one)
+            parts = []
+            total = None
+            for slot in range(SLOTS):
+                one = jnp.exp2(scores[:, slot * ROWS:(slot + 1) * ROWS] - (row_max + bias_ref[0, slot]))
+                part_sum = jnp.sum(one, axis=1, keepdims=True)
+                total = part_sum if total is None else total + part_sum
+                parts.append(one)
+            weights = jnp.concatenate(parts, axis=1)
+            inverse = 1.0 / total
+            attended = dot(weights.astype(BF), values) * inverse
+            attended = attended.astype(BF).astype(F32)
+            out = jnp.where(own_flat, attended, out)
+            up_own = jnp.where(own_flat, up_g, zero)
+            delta = jnp.sum(up_own.astype(F32) * attended, axis=1, keepdims=True)
+            dprobs = dot_t(up_own, values)
+            dscores = (weights * (dprobs - delta)).astype(BF)
+            dquery = jnp.where(own_pair, dot(dscores, keys) * (inverse * 0.125), dquery)
+            now = jnp.where(stat_lane == head, row_max + jnp.log2(total), now)
+            now = jnp.where(stat_lane == head + 4, delta, now)
+        out_ref[:, cols] = out.astype(BF)
+        dquery = turn_back(dquery, cos5[0], sin5[0]).astype(BF)
+        dq_ref[:, cols] = dot_t(dquery, perm).astype(BF)
+        stats_out[0, g] = now.T[:8]
+        for slot, peer in routes:
+            s_copy(g, slot, peer).start()
+
+        @pl.when(g > 0)
+        def _():
+            s_copy(g - 1, 2, near).wait_recv()
+            s_copy(g - 1, 4, partner).start()
+
+    s_copy(GROUPS - 1, 2, near).wait_recv()
+    s_copy(GROUPS - 1, 4, partner).start()
+    u_copies[2].wait()
+    u_copies[4].start()
+    u_copies[1].wait()
+    u_copies[3].wait()
+    keep_up.wait()
+
+    @pl.loop(0, GROUPS)
+    def _(g):
+        s_copy(g, 1, partner).wait()
+        s_copy(g, 2, near).wait_send()
+        s_copy(g, 3, ahead).wait()
+        s_copy(g, 4, partner).wait()
+
+    u_copies[4].wait()
+
+
+def key_kernel(bias_ref, stats_ref, q_ref, up_ref, k_ref, v_ref, cos_ref, sin_ref, dk_ref, dv_ref):
     perm = perm_matrix()
     lane = lanes((ROWS, 256))
     lane_pair = lane // 32 % 4
@@ -132,8 +242,8 @@
     for head in range(4):
         own_pair = lane_pair == head
         own_flat = lane_flat == head
-        lse = lse_ref[pl.ds(group * 4 + head, 1), :]
-        delta = delta_ref[pl.ds(group * 4 + head, 1), :]
+        lse = jnp.concatenate([stats_ref[slot, 0, head:head + 1] + bias_ref[0, slot] for slot in range(SLOTS)], axis=1)
+        delta = jnp.concatenate([stats_ref[slot, 0, head + 4:head + 5] for slot in range(SLOTS)], axis=1)
         scores = dot_t(jnp.where(own_pair, key, zero), q_ref[...]) * LOG2E
         probs = jnp.exp2(scores - lse)
         dprobs = dot_t(jnp.where(own_flat, value, zero), up_ref[...])
@@ -145,49 +255,53 @@
     dv_ref[...] = dvalue.astype(BF)
 
 
-def run_query(bias, x5, w, cos5, sin5, up):
-    full = lambda *shape: pl.BlockSpec(shape, lambda g: (0,) * len(shape))
-    col = lambda rows: pl.BlockSpec((rows, 256), lambda g: (0, g))
+def run_query(bias, x, w, up, spots, freq):
+    vmem = pl.BlockSpec(memory_space=pltpu.VMEM)
+    hbm = pl.BlockSpec(memory_space=pl.ANY)
+    dma = pltpu.SemaphoreType.DMA
     bf = lambda rows: jax.ShapeDtypeStruct((rows, 1024), BF)
     return pl.pallas_call(
         query_kernel,
-        grid=(GROUPS,),
-        in_specs=[
-            pl.BlockSpec(memory_space=pltpu.SMEM),
-            full(SLOTS, ROWS, 1024),
-            pl.BlockSpec((1024, 256), lambda g: (0, g)),
-            pl.BlockSpec((1024, 256), lambda g: (0, g + 4)),
-            pl.BlockSpec((1024, 256), lambda g: (0, g + 8)),
-            full(SLOTS, ROWS, 128),
-            full(SLOTS, ROWS, 128),
-            col(ROWS),
+        in_specs=[pl.BlockSpec(memory_space=pltpu.SMEM), hbm, hbm, hbm, vmem, vmem],
+        out_specs=[vmem, vmem, vmem, vmem, vmem, vmem, vmem, hbm, vmem],
+        out_shape=[bf(ROWS), bf(ROWS), bf(SLOTS * ROWS), bf(ROWS), bf(ROWS),
+                   jax.ShapeDtypeStruct((ROWS, 128), F32), jax.ShapeDtypeStruct((ROWS, 128), F32),
+                   bf(SLOTS * ROWS), jax.ShapeDtypeStruct((SLOTS, GROUPS, 8, ROWS), F32)],
+        scratch_shapes=[
+            pltpu.VMEM((SLOTS, ROWS, 1024), BF),
+            pltpu.VMEM((SLOTS, 8, ROWS), F32),
+            pltpu.VMEM((1024, 3072), BF),
+            pltpu.VMEM((1024, 2048), BF),
+            pltpu.VMEM((ROWS, 1024), BF),
+            pltpu.VMEM((SLOTS * ROWS, 1024), BF),
+            pltpu.VMEM((SLOTS * ROWS, 1024), BF),
+            pltpu.VMEM((SLOTS, ROWS, 128), F32),
+            pltpu.VMEM((SLOTS, ROWS, 128), F32),
+            dma((4,)), dma((5,)), dma((5,)), dma((5,)), dma((5,)), dma((5,)), dma((5,)),
+            dma((5, GROUPS)), dma((5, GROUPS)),
         ],
-        out_specs=[col(ROWS), col(ROWS), col(SLOTS * ROWS), col(ROWS), col(ROWS), full(2 * HEADS, ROWS)],
-        out_shape=[bf(ROWS), bf(ROWS), bf(SLOTS * ROWS), bf(ROWS), bf(ROWS),
-                   jax.ShapeDtypeStruct((2 * HEADS, ROWS), F32)],
-        scratch_shapes=[pltpu.VMEM((SLOTS * ROWS, 256), BF), pltpu.VMEM((SLOTS * ROWS, 256), BF),
-                        pltpu.VMEM((ROWS, 128), F32)],
-        compiler_params=pltpu.CompilerParams(vmem_limit_bytes=60 * 2**20),
+        compiler_params=pltpu.CompilerParams(collective_id=1, has_side_effects=True, vmem_limit_bytes=60 * 2**20),
         cost_estimate=pl.CostEstimate(flops=30 * 10**9, bytes_accessed=12 * 2**20, transcendentals=5 * 2**20),
         name="query_side",
-    )(bias, x5, w, w, w, cos5, sin5, up)
-
-
-def run_key(lse, delta, q5, up5, k, v, cosine, sine):
+    )(bias, x, w, up, spots, freq)
+
+
+def run_key(bias, stats, q5, up5, k, v, cosine, sine):
     full = lambda *shape: pl.BlockSpec(shape, lambda g: (0,) * len(shape))
     col = lambda rows: pl.BlockSpec((rows, 256), lambda g: (0, g))
     bf = lambda rows: jax.ShapeDtypeStruct((rows, 1024), BF)
     return pl.pallas_call(
         key_kernel,
         grid=(GROUPS,),
-        in_specs=[full(HEADS, SLOTS * ROWS), full(HEADS, SLOTS * ROWS), col(SLOTS * ROWS), col(SLOTS * ROWS),
+        in_specs=[pl.BlockSpec(memory_space=pltpu.SMEM), pl.BlockSpec((SLOTS, 1, 8, ROWS), lambda g: (0, g, 0, 0)),
+                  col(SLOTS * ROWS), col(SLOTS * ROWS),
                   col(ROWS), col(ROWS), full(ROWS, 128), full(ROWS, 128)],
         out_specs=[col(ROWS), col(ROWS)],
         out_shape=[bf(ROWS), bf(ROWS)],
         compiler_params=pltpu.CompilerParams(vmem_limit_bytes=60 * 2**20),
         cost_estimate=pl.CostEstimate(flops=12 * 10**9, bytes_accessed=8 * 2**20, transcendentals=5 * 2**20),
         name="key_side",
-    )(lse, delta, q5, up5, k, v, cosine, sine)
+    )(bias, stats, q5, up5, k, v, cosine, sine)
 
 
 def weight_kernel(x_ref, d_ref, g_ref):
@@ -311,16 +425,6 @@
 
 
 SWAP = [(i, i ^ 1) for i in range(N_LON)]
-NEAR = [(i, (i + (1 if i % 2 else -1)) % N_LON) for i in range(N_LON)]
-WIDE = [(i, (i + (-2 if i % 2 else 2)) % N_LON) for i in range(N_LON)]
-
-
-def gather_halo(value):
-    partner = lax.ppermute(value, "lon", SWAP)
-    near = lax.ppermute(value, "lon", NEAR)
-    wide = lax.ppermute(value, "lon", WIDE)
-    passed = lax.ppermute(near, "lon", SWAP)
-    return [value, partner, near, wide, passed]
 
 
 def per_device(features, w_qkv, grad_out, positions, block_list):
@@ -332,26 +436,18 @@
     used = jnp.any(listed[None, :] == offsets[:, None], axis=1)
     used_by = jnp.any(listed[None, :] == -offsets[:, None], axis=1)
     bias = jnp.where(used, 0.0, FAR).astype(F32).reshape(1, SLOTS)
-
+    bias_by = jnp.where(used_by, 0.0, FAR).astype(F32).reshape(1, SLOTS)
     pair_index = jnp.arange(32, dtype=F32)
     frequency = INTERP * BASE ** (-2.0 * pair_index / 64)
-    spots = jnp.concatenate(gather_halo(positions), axis=0)
-    angles = spots.astype(F32)[..., None] * frequency
-    cos5 = jnp.tile(jnp.cos(angles), (1, 1, 4))
-    sin5 = jnp.tile(jnp.sin(angles), (1, 1, 4))
-    x5 = jnp.stack(gather_halo(x))
-    up5 = jnp.concatenate(gather_halo(up), axis=0)
-    out, dq, q5, k, v, stats = run_query(bias, x5, w_qkv, cos5, sin5, up)
-    stats5 = jnp.stack(gather_halo(stats))
-    lse = stats5[:, :HEADS] + jnp.where(used_by, 0.0, FAR)[:, None, None]
-    delta = stats5[:, HEADS:]
-    lse = jnp.transpose(lse, (1, 0, 2)).reshape(HEADS, SLOTS * ROWS)
-    delta = jnp.transpose(delta, (1, 0, 2)).reshape(HEADS, SLOTS * ROWS)
-    dk, dv = run_key(lse, delta, q5, up5, k, v, cos5[0], sin5[0])
+    freq = jnp.broadcast_to(jnp.tile(frequency, 4)[None], (8, 128))
+    spots = jnp.broadcast_to(positions.astype(F32), (8, ROWS))
+    out, dq, q5, k, v, cosine, sine, up5, stats = run_query(bias, x, w_qkv, up, spots, freq)
+    dk, dv = run_key(bias_by, stats, q5, up5, k, v, cosine, sine)
     dqkv = jnp.concatenate([dq, dk, dv], axis=1)
     d_other = lax.ppermute(dqkv, "lon", SWAP)
+    x_other = lax.ppermute(x, "lon", SWAP)
     grad_x = lax.dot_general(dqkv, w_qkv, (((1,), (1,)), ((), ())), preferred_element_type=F32).astype(BF)
-    tokens = x5[:2].reshape(2 * ROWS, 16, 2, 32)
+    tokens = jnp.concatenate([x, x_other], axis=0).reshape(2 * ROWS, 16, 2, 32)
     x_rows = lax.dynamic_index_in_dim(tokens, core, axis=2, keepdims=False).reshape(2 * ROWS, 512).T
     partial = run_weight(x_rows, jnp.concatenate([dqkv, d_other], axis=0))
     grad_w = run_reduce(partial)

time: 186 us -> 159 us (0.85)
  Pallas kernels: 100 us -> 134 us
  waiting for transfers between devices: 25.3 us -> 0.01 us
  local copies, waits for them, and re-layouts: 30.1 us -> 8.38 us
  starting transfers between devices: 14.1 us -> 1.13 us
    pallas_call x2, Pallas kernels: 49.7 us -> 83.9 us  [the longest x1 68.1 us: run_query(): pl.pallas_call(query_kernel, in_specs=[pl.BlockSpec(memory_space=pltpu.SM...]
    ppermute x16 -> x1, waiting for transfers between devices: 25.3 us -> 0.01 us  [per_device(): x_other = lax.ppermute(x, 'lon', SWAP)]
    ppermute x16 -> x1, starting transfers between devices: 13.9 us -> 0.11 us  [per_device(): x_other = lax.ppermute(x, 'lon', SWAP)]
    unnamed x19 -> x11, local copies, waits for them, and re-layouts: 18 us -> 5.74 us
    another operation x11 -> x1, local copies, waits for them, and re-layouts: 5.7 us -> 0.01 us  [per_device(): freq = jnp.broadcast_to(jnp.tile(frequency, 4)[None], (8, 128))]
    reshape x3 -> x0, local copies, waits for them, and re-layouts: 1.98 us -> none  [the longest x1 0.71 us: per_device(): tokens = x5[:2].reshape(2 * ROWS, 16, 2, 32)]
  transfers between devices with their start and end apart: 17 -> 2, of which waited for: 4 -> 0; matrix products, arithmetic and copies ran while one was open for 17% -> 4% of each run, Pallas kernels for 19% -> 0%
where the time goes in v2:
time: 159 us; the launch traced here: 156 us
  Pallas kernels  134 us (84%)
  local copies, waits for them, and re-layouts  8.38 us (5%)
  other arithmetic  6.23 us (4%)
  matrix products  5.4 us (3%)
    pallas_call x1, Pallas kernels, run_query(): pl.pallas_call(query_kernel, in_specs=[pl.BlockSpec(memory_space=pltpu.SM...  68.1 us
    pallas_call x1, Pallas kernels, run_reduce(): pl.pallas_call(reduce_kernel, in_specs=[pl.BlockSpec(memory_space=pltpu.V...  42.2 us
    pallas_call x1, Pallas kernels, run_key(): pl.pallas_call(key_kernel, grid=(GROUPS,), in_specs=[pl.BlockSpec(memory_...  15.8 us
    pallas_call x1, Pallas kernels, run_weight(): pl.pallas_call(weight_kernel, grid=(8,), in_specs=[pl.BlockSpec((512, 512...  7.79 us
    unnamed x11, local copies, waits for them, and re-layouts  5.74 us
    dot_general x1, matrix products, per_device(): lax.dot_general(dqkv, w_qkv, (((1,), (1,)), ((), ())), preferred_element_...  5.4 us
    concatenate x1, other arithmetic, per_device(): partial = run_weight(x_rows, jnp.concatenate([dqkv, d_other], axis=0))  3.26 us
  transfers between devices with their start and end apart: 2, of which 0 were waited for; matrix products, arithmetic and copies ran while one was open for 4% of the time, Pallas kernels for 0%

profile of v2, /device:TPU:7, one launch (start us, length us, event | category | flops | bytes accessed | tf_op | source)
XLA Modules:
  0.0 155.7 jit_solution(13248734173521579362)
XLA Ops:
  0.7 0.1 stack.19
  0.8 0.7 convert_element_type.6
  1.4 0.1 broadcast_in_dim.36
  1.5 0.9 compare_reduce_fusion
  2.4 0.6 select_bitcast_fusion
  2.9 0.6 broadcast_in_dim.35.spots_ref
  3.5 0.6 broadcast_in_dim.37.freq_ref
  4.1 68.1 %query_side.1 = (bf16[256,1024]{1,0:T(8,128)(2,1)}, bf16[256,1024]{1,0:T(8,128)(2,1)}, bf16[1280,1024]{1,0:T(8,128)(2,1)}, bf16[256,1024]{1,0:T(8,128)(2,1)}, bf...) custom-call(f32[1,5]{1,0:T(1,128)} %get-tuple-element.28.bias_ref, ...), custom_call_target="tpu_custom_call" | custom-call | flops 30000001024 | bytes 12582912 | tf_op jit(solution)/shard_map/query_side/pallas_call | solution.py:263
  72.2 1.1 constant_dynamic-update-slice_fusion.2
  73.3 15.8 %key_side.1 = (bf16[256,1024]{1,0:T(8,128)(2,1)}, bf16[256,1024]{1,0:T(8,128)(2,1)}) custom-call(f32[1,5]{1,0:T(1,128)} %get-tuple-element.27.bias_ref, f32[5,4,8,256]{3,2,1,0:T(8,128)} %get-tuple-element.16.stats_ref, bf16[1280,1024]{1,0:T(8,128)(2,1)} %get-tuple-element.17.q_ref, bf16[1280,1024]{1,0:T(8,128)(2,1)} %get-tuple-element.18.up_ref, ...), custom_call_target="tpu_custom_call" | custom-call | flops 12000000000 | bytes 8388608 | tf_op jit(solution)/shard_map/key_side/pallas_call | solution.py:293
  89.1 0.0 copy-start.1
  89.1 1.1 constant_dynamic-update-slice_fusion.1
  90.2 1.1 constant_dynamic-update-slice_fusion
  91.3 1.0 collective-permute-start.1
  92.3 0.0 copy-done.1
  92.3 0.1 collective-permute-start
  92.5 0.2 copy.12
  92.7 5.4 %fusion = bf16[1,256,1024]{2,1,0:T(8,128)(2,1)} fusion(bf16[256,3072]{1,0:T(8,128)(2,1)S(1)} %constant_dynamic-update-slice_fusion, bf16[1024,3072]{1,0:T(8,128)(2,1)} %w_hbm.1), kind=kOutput, calls=%fused_computation.2 | convolution fusion | flops 1610874880 | bytes 8388608 | tf_op jit(solution)/shard_map/dot_general | solution.py:449
  98.1 0.0 collective-permute-done
  98.1 0.2 copy.13
  98.3 0.8 fusion.1
  99.1 0.0 collective-permute-done.1
  99.1 3.3 %pad_maximum_fusion.d_ref = bf16[512,3072]{1,0:T(8,128)(2,1)} fusion(bf16[256,3072]{1,0:T(8,128)(2,1)} %collective-permute-done.1, bf16[256,3072]{1,0:T(8,128)(2,1)S(1)} %constant_dynamic-update-slice_fusion), kind=kLoop, calls=%fused_computation | loop fusion | flops 6291456 | bytes 6291456 | tf_op jit(solution)/shard_map/concatenate | solution.py:452
  102.4 7.8 %weight_partial.1 = bf16[8,512,384]{2,1,0:T(8,128)(2,1)} custom-call(bf16[512,512]{1,0:T(8,128)(2,1)} %bitcast.26, bf16[512,3072]{1,0:T(8,128)(2,1)} %pad_maximum_fusion.d_ref), custom_call_target="tpu_custom_call" | custom-call | tf_op jit(solution)/shard_map/weight_partial/pallas_call | solution.py:312
  110.2 0.0 copy-start
  110.2 1.9 %copy-done = bf16[8,512,384]{2,1,0:T(8,128)(2,1)S(1)} copy-done((bf16[8,512,384]{2,1,0:T(8,128)(2,1)S(1)}, bf16[8,512,384]{2,1,0:T(8,128)(2,1)}, u32[]{:S(2)}) %copy-start) | copy-done | bytes 3145752
  112.1 0.0 copy-start.2
  112.1 42.2 %weight_reduce.1 = f32[64,192]{1,0:T(8,128)S(1)} custom-call(bf16[4,2,8,2,32,384]{5,4,3,2,1,0:T(8,128)(2,1)S(1)} %bitcast.23), custom_call_target="tpu_custom_call" | custom-call | tf_op jit(solution)/shard_map/weight_reduce/pallas_call | solution.py:403
  154.3 0.0 copy-done.2
  154.3 0.8 copy.18
  155.1 0.6 copy.19
  (3 shorter events, 0.0 us)
Async XLA Ops:
  89.1 3.3 %copy-start.1 = (bf16[1,256,1024]{2,1,0:T(8,128)(2,1)S(1)}, bf16[1,256,1024]{2,1,0:T(8,128)(2,1)}, u32[]{:S(2)}) copy-start(bf16[1,256,1024]{2,1,0:T(8,128)(2,1)} %param.5) | copy-start | bytes 1572868
  91.3 7.8 %collective-permute-start.1 = (bf16[256,3072]{1,0:T(8,128)(2,1)S(1)}, bf16[256,3072]{1,0:T(8,128)(2,1)}, u32[]{:S(2)}, u32[]{:S(2)}) collective-permute-start(bf16[256,3072]{1,0:T(8,128)(2,1)S(1)} %constant_dynamic-update-slice_fusion), channel_id=1, source_target_pairs={{0,16},{16,0},{32,48},{48,32},{64,80},{80,64},{96,112},{112,96},{1... | collective-permute-start | bytes 4718600 | tf_op jit(solution)/shard_map/ppermute | solution.py:447
  92.3 5.7 %collective-permute-start = (bf16[256,1024]{1,0:T(8,128)(2,1)S(1)}, bf16[256,1024]{1,0:T(8,128)(2,1)S(1)}, u32[]{:S(2)}, u32[]{:S(2)}) collective-permute-start(bf16[256,1024]{1,0:T(8,128)(2,1)S(1)} %bitcast.28), channel_id=1, source_target_pairs={{0,16},{16,0},{32,48},{48,32},{64,80},{80,64},{96,112},{112,96},{1... | collective-permute-start | bytes 1572872 | tf_op jit(solution)/shard_map/ppermute | solution.py:448
  110.2 1.9 %copy-start = (bf16[8,512,384]{2,1,0:T(8,128)(2,1)S(1)}, bf16[8,512,384]{2,1,0:T(8,128)(2,1)}, u32[]{:S(2)}) copy-start(bf16[8,512,384]{2,1,0:T(8,128)(2,1)} %weight_partial.1) | copy-start | bytes 9437188
  112.1 42.2 %copy-start.2 = (bf16[256,1024]{1,0:T(8,128)(2,1)S(1)}, bf16[256,1024]{1,0:T(8,128)(2,1)}, u32[]{:S(2)}) copy-start(bf16[256,1024]{1,0:T(8,128)(2,1)} %get-tuple-element.14) | copy-start | bytes 1572868

commit v3 on v2

v3 whole, which is shorter than its diff:
```python
import jax
import jax.numpy as jnp
from jax import lax
from jax.experimental import pallas as pl
from jax.experimental.pallas import tpu as pltpu
from jax.sharding import PartitionSpec as P

INTERP = 0.25
BASE = 10000.0
FAR = 1e30
LOG2E = 1.4426950408889634
BF = jnp.bfloat16
F32 = jnp.float32
MESH = pl.DeviceIdType.MESH
ROWS = 256
GROUPS = 4
SLOTS = 5
PIECES = 4


def dot(a, b):
    return lax.dot_general(a, b, (((1,), (0,)), ((), ())), preferred_element_type=F32)


def dot_t(a, b):
    return lax.dot_general(a, b, (((1,), (1,)), ((), ())), preferred_element_type=F32)


def lanes(shape):
    return lax.broadcasted_iota(jnp.int32, shape, len(shape) - 1)


def perm_matrix():
    source = lax.broadcasted_iota(jnp.int32, (256, 256), 0)
    column = lax.broadcasted_iota(jnp.int32, (256, 256), 1)
    wanted = (column // 32 % 4) * 64 + (column // 128) * 32 + column % 32
    return jnp.where(source == wanted, 1.0, 0.0).astype(BF)


def turn(value, cosine, sine):
    a, c = value[:, :128], value[:, 128:]
    return jnp.concatenate([a * cosine - c * sine, a * sine + c * cosine], axis=1)


def turn_back(value, cosine, sine):
    a, c = value[:, :128], value[:, 128:]
    return jnp.concatenate([a * cosine + c * sine, c * cosine - a * sine], axis=1)


def step_kernel(bias_ref, x_hbm, w_hbm, up_hbm, spots_ref, freq_ref,
                out_ref, gx_ref, gw_ref,
                perm_ref, xs, spots, wbuf, wpair, upbuf, qbuf, kbuf, vbuf, cos5, sin5, stats, both, xt,
                g_buf, in_x, in_y, sum_a, sum_b, in_a, in_b, sum_p, in_z, mine, theirs,
                local, x_send, x_recv, p_send, p_recv, u_send, u_recv, s_send, s_recv, d_send, d_recv,
                send_x, recv_x, send_y, recv_y, send_a, recv_a, send_b, recv_b, send_z, recv_z, send_c, recv_c):
    lon, dates = lax.axis_index("lon"), lax.axis_index("dates")
    x, y_lo, core = lon // 4, lax.rem(lon // 2, 2), lax.rem(lon, 2)
    z, y_hi = dates // 2, lax.rem(dates, 2)
    y = y_hi * 2 + y_lo
    step = 1 - 2 * y_lo

    def at(px, py, pz, pc):
        return {"lon": lax.rem(px + 4, 4) * 4 + lax.rem(py, 2) * 2 + pc, "dates": pz * 2 + py // 2}

    other_y = y_hi * 2 + 1 - y_lo
    partner = at(x, y, z, 1 - core)
    pair = at(x, other_y, z, core)
    onward = at(x + step, y, z, core)
    diagonal = at(x - step, other_y, z, core)
    passing = 2 + lax.rem(core + y_lo, 2)
    x_peers = [lax.rem(x + i, 4) for i in (1, 2, 3)]
    y_peers = [lax.rem(y + i, 4) for i in (1, 2, 3)]
    z_peers = [lax.rem(z + i, 8) for i in range(1, 8)]

    bring = [pltpu.make_async_copy(x_hbm, xs.at[0], local.at[0]),
             pltpu.make_async_copy(w_hbm, wbuf, local.at[1]),
             pltpu.make_async_copy(up_hbm, upbuf.at[pl.ds(0, ROWS)], local.at[2])]
    for copy in bring:
        copy.start()
    barrier = pltpu.get_barrier_semaphore()
    peers = [partner, diagonal] + [at(p, y, z, core) for p in x_peers] + [at(x, p, z, core) for p in y_peers]
    peers += [at(x, y, p, core) for p in z_peers]
    for peer in peers:
        pl.semaphore_signal(barrier, inc=1, device_id=peer, device_id_type=MESH)
    pl.semaphore_wait(barrier, len(peers))

    def remote(source, target, send_sem, recv_sem, peer):
        return pltpu.make_async_remote_copy(src_ref=source, dst_ref=target, send_sem=send_sem, recv_sem=recv_sem,
                                            device_id=peer, device_id_type=MESH)

    routes = ((1, partner), (2, pair), (3, diagonal))
    p_copies = {slot: remote(spots_ref, spots.at[slot], p_send.at[slot], p_recv.at[slot], peer) for slot, peer in routes}
    p_copies[4] = remote(spots.at[passing], spots.at[4], p_send.at[4], p_recv.at[4], partner)

    def piece(j):
        return pl.ds(j * (ROWS // PIECES), ROWS // PIECES)

    x_partner = remote(x_hbm, xs.at[1], x_send.at[0], x_recv.at[0], partner)
    x_pass = remote(xs.at[passing], xs.at[4], x_send.at[1], x_recv.at[1], partner)
    x_pair = [remote(x_hbm.at[piece(j)], xs.at[2, piece(j)], x_send.at[2 + j], x_recv.at[2 + j], pair)
              for j in range(PIECES)]
    x_cross = [remote(xs.at[2, piece(j)], xs.at[3, piece(j)], x_send.at[2 + PIECES + j], x_recv.at[2 + PIECES + j], onward)
               for j in range(PIECES)]

    def block(slot):
        return pl.ds(pl.multiple_of(slot * ROWS, ROWS), ROWS)

    u_copies = {slot: remote(up_hbm, upbuf.at[block(slot)], u_send.at[slot], u_recv.at[slot], peer)
                for slot, peer in routes[:2]}
    u_copies[3] = remote(upbuf.at[block(2)], upbuf.at[block(3)], u_send.at[3], u_recv.at[3], onward)
    u_copies[4] = remote(upbuf.at[block(passing)], upbuf.at[block(4)], u_send.at[4], u_recv.at[4], partner)
    for slot in (1, 2, 3):
        p_copies[slot].start()
    for copy in x_pair:
        copy.start()
    x_partner.start()
    u_copies[2].start()
    u_copies[1].start()

    perm_ref[...] = perm_matrix()
    bring[0].wait()
    bring[1].wait()

    def cols(part, g):
        return pl.ds(pl.multiple_of(part * 1024 + g * 256, 256), 256)

    @pl.loop(0, 2 * GROUPS)
    def _(g):
        wpair[:, cols(0, g)] = dot(wbuf[:, cols(0, g)], perm_ref[...]).astype(BF)

    def tables(slot, row):
        spread = jnp.broadcast_to(row, (128, ROWS)).T
        angle = spread * freq_ref[0:1, :]
        cos5[slot] = jnp.cos(angle)
        sin5[slot] = jnp.sin(angle)

    def project(slot):
        @pl.loop(0, GROUPS)
        def _(g):
            tokens = xs[slot]
            cosine, sine = cos5[slot], sin5[slot]
            query = turn(dot(tokens, wpair[:, cols(0, g)]), cosine, sine).astype(BF).astype(F32) * 0.125
            qbuf[block(slot), cols(0, g)] = query.astype(BF)
            kbuf[block(slot), cols(0, g)] = turn(dot(tokens, wpair[:, cols(1, g)]), cosine, sine).astype(BF)
            vbuf[block(slot), cols(0, g)] = dot(tokens, wbuf[:, cols(2, g)]).astype(BF)

    def hand_on(j):
        x_pair[j].wait_recv()
        x_cross[j].start()

    def stripes(slot):
        row = lax.broadcasted_iota(jnp.int32, (128, 256), 0)
        chosen = lanes((128, 256)) == row // 32 * 64 + core * 32 + row % 32
        select = jnp.where(chosen, 1.0, 0.0).astype(BF)
        for g in range(GROUPS):
            xt[g * 128:(g + 1) * 128, slot * ROWS:(slot + 1) * ROWS] = dot_t(select, xs[slot, :, g * 256:(g + 1) * 256]).astype(BF)

    hand_on(0)
    tables(0, spots_ref[0:1, :])
    project(0)
    hand_on(1)
    p_copies[1].wait()
    tables(1, spots[1, 0:1, :])
    x_partner.wait()
    project(1)
    hand_on(2)
    p_copies[2].wait()
    p_copies[3].wait()
    p_copies[4].start()
    tables(2, spots[2, 0:1, :])
    tables(3, spots[3, 0:1, :])
    hand_on(3)
    project(2)
    p_copies[4].wait()
    tables(4, spots[4, 0:1, :])
    stripes(0)
    stripes(1)
    for copy in x_cross:
        copy.wait()
    x_pass.start()
    project(3)
    for copy in x_pair:
        copy.wait_send()
    bring[2].wait()
    x_pass.wait()
    project(4)
    lane = lanes((ROWS, 256))
    lane_pair = lane // 32 % 4
    lane_flat = lane // 64
    stat_lane = lanes((ROWS, 128))
    zero = jnp.zeros((), BF)

    def s_copy(g, slot, peer):
        return remote(stats.at[passing if slot == 4 else 0, g], stats.at[slot, g],
                      s_send.at[slot, g], s_recv.at[slot, g], peer)

    def d_copy(part, g):
        return remote(both.at[pl.ds(0, ROWS), cols(part, g)], both.at[pl.ds(ROWS, ROWS), cols(part, g)],
                      d_send.at[part, g], d_recv.at[part, g], partner)

    @pl.loop(0, GROUPS)
    def _(g):
        mid = cols(0, g)
        query = qbuf[block(0), mid]
        up_g = upbuf[block(0), mid]
        out = jnp.zeros((ROWS, 256), F32)
        dquery = jnp.zeros((ROWS, 256), F32)
        now = jnp.zeros((ROWS, 128), F32)
        for head in range(4):
            own_pair = lane_pair == head
            own_flat = lane_flat == head
            scores = dot_t(jnp.where(own_pair, query, zero), kbuf[:, mid]) * LOG2E
            row_max = None
            for slot in range(SLOTS):
                one = jnp.max(scores[:, slot * ROWS:(slot + 1) * ROWS], axis=1, keepdims=True) - bias_ref[0, slot]
                row_max = one if row_max is None else jnp.maximum(row_max, one)
            parts = []
            total = None
            for slot in range(SLOTS):
                one = jnp.exp2(scores[:, slot * ROWS:(slot + 1) * ROWS] - (row_max + bias_ref[0, slot]))
                part_sum = jnp.sum(one, axis=1, keepdims=True)
                total = part_sum if total is None else total + part_sum
                parts.append(one)
            weights = jnp.concatenate(parts, axis=1)
            inverse = 1.0 / total
            attended = dot(weights.astype(BF), vbuf[:, mid]) * inverse
            attended = attended.astype(BF).astype(F32)
            out = jnp.where(own_flat, attended, out)
            up_own = jnp.where(own_flat, up_g, zero)
            delta = jnp.sum(up_own.astype(F32) * attended, axis=1, keepdims=True)
            dprobs = dot_t(up_own, vbuf[:, mid])
            dscores = (weights * (dprobs - delta)).astype(BF)
            dquery = jnp.where(own_pair, dot(dscores, kbuf[:, mid]) * (inverse * 0.125), dquery)
            now = jnp.where(stat_lane == head, row_max + jnp.log2(total), now)
            now = jnp.where(stat_lane == head + 4, delta, now)
        stats[0, g] = now.T[:8]
        dquery = turn_back(dquery, cos5[0], sin5[0]).astype(BF)
        both[0:ROWS, mid] = dot_t(dquery, perm_ref[...]).astype(BF)
        out_ref[:, mid] = out.astype(BF)
        for slot, peer in routes:
            s_copy(g, slot, peer).start()
        d_copy(0, g).start()

        def pass_stats(g):
            s_copy(g, 2, pair).wait_recv()
            s_copy(g, 3, diagonal).wait_recv()
            s_copy(g, 4, partner).start()

        @pl.when(g > 0)
        def _():
            pass_stats(g - 1)

        @pl.when(g == 0)
        def _():
            u_copies[2].wait_recv()
            u_copies[3].start()

        @pl.when(g == 2)
        def _():
            u_copies[3].wait_recv()
            u_copies[4].start()

        @pl.when(g == GROUPS - 1)
        def _():
            pass_stats(g)

    def send_first(s):
        px, lo = s // 6, lax.rem(s // 3, 2)

        @pl.when(px != x)
        def _():
            slot = lax.rem(px - x + 3, 4)
            remote(g_buf.at[s, pl.ds(0, 4)], in_x.at[slot, s - 6 * px], send_x.at[slot], recv_x.at[slot],
                   at(px, y, z, core)).start()

        for hi in range(2):
            py = hi * 2 + lo

            @pl.when(py != y)
            def _():
                slot = lax.rem(py - y + 3, 4)
                remote(g_buf.at[s, pl.ds(4, 4), hi], in_y.at[slot, px * 3 + lax.rem(s, 3)], send_y.at[slot],
                       recv_y.at[slot], at(x, py, z, core)).start()

    def weight_piece(part, g):
        d_copy(part, g).wait_recv()
        value = dot(xt[...], both[:, cols(part, g)]).astype(BF)
        first = part * 8 + g * 2
        g_buf[first] = value[:, :128].reshape(8, 2, 32, 128)
        g_buf[first + 1] = value[:, 128:].reshape(8, 2, 32, 128)
        send_first(first)
        send_first(first + 1)

    @pl.loop(0, GROUPS)
    def _(g):
        mid = cols(0, g)
        s_copy(g, 1, partner).wait_recv()
        s_copy(g, 4, partner).wait_recv()

        @pl.when(g == 0)
        def _():
            u_copies[1].wait_recv()
            u_copies[4].wait_recv()

        weight_piece(0, g)
        key, value = kbuf[block(0), mid], vbuf[block(0), mid]
        dkey = jnp.zeros((ROWS, 256), F32)
        dvalue = jnp.zeros((ROWS, 256), F32)
        for head in range(4):
            own_pair = lane_pair == head
            own_flat = lane_flat == head
            lse = jnp.concatenate([stats[slot, g, head:head + 1] + bias_ref[1, slot] for slot in range(SLOTS)], axis=1)
            delta = jnp.concatenate([stats[slot, g, head + 4:head + 5] for slot in range(SLOTS)], axis=1)
            scores = dot_t(jnp.where(own_pair, key, zero), qbuf[:, mid]) * LOG2E
            probs = jnp.exp2(scores - lse)
            dprobs = dot_t(jnp.where(own_flat, value, zero), upbuf[:, mid])
            dscores = (probs * (dprobs - delta)).astype(BF)
            dvalue = jnp.where(own_flat, dot(probs.astype(BF), upbuf[:, mid]), dvalue)
            dkey = jnp.where(own_pair, dot(dscores, qbuf[:, mid]), dkey)
        dkey = turn_back(dkey, cos5[0], sin5[0]).astype(BF)
        both[0:ROWS, cols(2, g)] = dvalue.astype(BF)
        both[0:ROWS, cols(1, g)] = dot_t(dkey, perm_ref[...]).astype(BF)
        d_copy(2, g).start()
        d_copy(1, g).start()

        @pl.when(g > 0)
        def _():
            weight_piece(2, g - 1)
            weight_piece(1, g - 1)

    weight_piece(2, GROUPS - 1)
    weight_piece(1, GROUPS - 1)

    def grad_x(j):
        rows = slice(j * 256, (j + 1) * 256)
        gx_ref[:, rows] = dot_t(both[0:ROWS], wbuf[rows]).astype(BF)

    grad_x(0)
    grad_x(1)
    first_a = [remote(in_x.at[i], in_x.at[i], send_x.at[i], recv_x.at[i], at(p, y, z, core)) for i, p in enumerate(x_peers)]
    first_b = [remote(in_y.at[i], in_y.at[i], send_y.at[i], recv_y.at[i], at(x, p, z, core)) for i, p in enumerate(y_peers)]
    for copy in first_a:
        copy.wait_recv()
    for j in range(6):
        total = g_buf[6 * x + j, 0:4].astype(F32)
        for i in range(3):
            total += in_x[i, j].astype(F32)
        sum_a[j] = total.astype(BF)
    second_a = [remote(sum_a.at[pl.ds(lax.rem(p, 2) * 3, 3), :, p // 2], in_a.at[i], send_a.at[i], recv_a.at[i],
                       at(x, p, z, core)) for i, p in enumerate(y_peers)]
    for copy in second_a:
        copy.start()
    for copy in first_b:
        copy.wait_recv()
    for px in range(4):
        for j in range(3):
            total = g_buf[px * 6 + y_lo * 3 + j, 4:8, y_hi].astype(F32)
            for i in range(3):
                total += in_y[i, px * 3 + j].astype(F32)
            sum_b[px * 3 + j] = total.astype(BF)
    second_b = [remote(sum_b.at[pl.ds(p * 3, 3)], in_b.at[i], send_b.at[i], recv_b.at[i], at(p, y, z, core))
                for i, p in enumerate(x_peers)]
    for copy in second_b:
        copy.start()
    grad_x(2)
    for copy in second_a:
        copy.wait_recv()
    for j in range(3):
        total = sum_a[y_lo * 3 + j, :, y_hi].astype(F32)
        for i in range(3):
            total += in_a[i, j].astype(F32)
        sum_p[0:4, j] = total.astype(BF)
    for copy in second_b:
        copy.wait_recv()
    for j in range(3):
        total = sum_b[x * 3 + j].astype(F32)
        for i in range(3):
            total += in_b[i, j].astype(F32)
        sum_p[4:8, j] = total.astype(BF)
    third = [remote(sum_p.at[p], in_z.at[i], send_z.at[i], recv_z.at[i], at(x, y, p, core)) for i, p in enumerate(z_peers)]
    for copy in third:
        copy.start()
    grad_x(3)
    for copy in first_a + first_b + second_a + second_b:
        copy.wait_send()
    u_copies[1].wait_send()
    u_copies[2].wait_send()
    u_copies[3].wait_send()
    u_copies[4].wait_send()

    @pl.loop(0, GROUPS)
    def _(g):
        for part in range(3):
            d_copy(part, g).wait_send()
        s_copy(g, 1, partner).wait_send()
        s_copy(g, 2, pair).wait_send()
        s_copy(g, 3, diagonal).wait_send()
        s_copy(g, 4, partner).wait_send()

    for copy in third:
        copy.wait()
    pieces = []
    for j in range(3):
        total = sum_p[z, j].astype(F32)
        for i in range(7):
            total += in_z[i, j].astype(F32)
        pieces.append(total * (65536.0 ** -0.5))
    total = jnp.concatenate(pieces, axis=1)
    mine[0] = total[:, :192]
    mine[1] = total[:, 192:]
    last = remote(mine.at[1 - core], theirs, send_c, recv_c, partner)
    last.start()
    gw_ref[pl.ds(pl.multiple_of(core * 32, 32), 32), :] = mine[core]
    last.wait()
    gw_ref[pl.ds(pl.multiple_of(32 - core * 32, 32), 32), :] = theirs[...]


def run_step(bias, x, w, up, spots, freq):
    vmem = pl.BlockSpec(memory_space=pltpu.VMEM)
    hbm = pl.BlockSpec(memory_space=pl.ANY)
    dma = pltpu.SemaphoreType.DMA
    block = jax.ShapeDtypeStruct((ROWS, 1024), BF)
    buffers = [
        ((256, 256), BF), ((SLOTS, ROWS, 1024), BF), ((SLOTS, 8, ROWS), F32), ((1024, 3072), BF), ((1024, 2048), BF),
        ((SLOTS * ROWS, 1024), BF), ((SLOTS * ROWS, 1024), BF), ((SLOTS * ROWS, 1024), BF), ((SLOTS * ROWS, 1024), BF),
        ((SLOTS, ROWS, 128), F32), ((SLOTS, ROWS, 128), F32), ((SLOTS, GROUPS, 8, ROWS), F32),
        ((2 * ROWS, 3072), BF), ((512, 512), BF),
        ((24, 8, 2, 32, 128), BF), ((3, 6, 4, 2, 32, 128), BF), ((3, 12, 4, 32, 128), BF), ((6, 4, 2, 32, 128), BF),
        ((12, 4, 32, 128), BF), ((3, 3, 4, 32, 128), BF), ((3, 3, 4, 32, 128), BF), ((8, 3, 32, 128), BF),
        ((7, 3, 32, 128), BF), ((2, 32, 192), F32), ((32, 192), F32),
    ]
    moves = (2 + 2 * PIECES,)
    semaphores = [dma((3,)), dma(moves), dma(moves)] + [dma((5,))] * 4 + [dma((5, GROUPS))] * 2 + [dma((3, GROUPS))] * 2
    semaphores += [dma((3,))] * 8 + [dma((7,))] * 2 + [dma, dma]
    return pl.pallas_call(
        step_kernel,
        in_specs=[pl.BlockSpec(memory_space=pltpu.SMEM), hbm, hbm, hbm, vmem, vmem],
        out_specs=[vmem, vmem, vmem],
        out_shape=[block, block, jax.ShapeDtypeStruct((64, 192), F32)],
        scratch_shapes=[pltpu.VMEM(shape, kind) for shape, kind in buffers] + semaphores,
        compiler_params=pltpu.CompilerParams(collective_id=0, has_side_effects=True, vmem_limit_bytes=63 * 2**20),
        name="whole_step",
    )(bias, x, w, up, spots, freq)


def per_device(features, w_qkv, grad_out, positions, block_list):
    lon = lax.axis_index("lon")
    toward, step = 1 - 2 * (lon % 2), 1 - 2 * (lon // 2 % 2)
    offsets = jnp.stack([jnp.int32(0), toward, 2 * step, -2 * step, -toward])
    sides = jnp.stack([offsets, -offsets])
    used = jnp.any(block_list[0][None, None, :] == sides[:, :, None], axis=2)
    bias = jnp.where(used, 0.0, FAR).astype(F32)
    pair_index = jnp.arange(32, dtype=F32)
    frequency = INTERP * BASE ** (-2.0 * pair_index / 64)
    freq = jnp.broadcast_to(jnp.tile(frequency, 4)[None], (8, 128))
    spots = jnp.broadcast_to(positions.astype(F32), (8, ROWS))
    out, grad_x, grad_w = run_step(bias, features[0], w_qkv, grad_out[0], spots, freq)
    return (out[None], grad_x[None], grad_w)


def solution(mesh):
    return jax.shard_map(
        per_device,
        mesh=mesh,
        in_specs=(
            P("dates", "lon", None),
            P(),
            P("dates", "lon", None),
            P("dates", "lon"),
            P("dates", None),
        ),
        out_specs=(P("dates", "lon", None), P("dates", "lon", None), P("dates", "lon")),
        check_vma=False,
    )
```

time: 159 us -> 117 us (0.74); the launches traced: 156 us -> 115 us
  Pallas kernels: 134 us -> 106 us
  matrix products: 5.4 us -> 0 us
  other arithmetic: 6.23 us -> 2.16 us
  local copies, waits for them, and re-layouts: 8.38 us -> 6.68 us
    pallas_call x4 -> x1, Pallas kernels: 134 us -> 106 us  [run_step(): pl.pallas_call(step_kernel, in_specs=[pl.BlockSpec(memory_space=pltpu.SME...]
    dot_general x1 -> x0, matrix products: 5.4 us -> none  [per_device(): lax.dot_general(dqkv, w_qkv, (((1,), (1,)), ((), ())), preferred_element_...]
    concatenate x2 -> x0, other arithmetic: 4.11 us -> none  [the longest x1 3.26 us: per_device(): partial = run_weight(x_rows, jnp.concatenate([dqkv, d_other], axis=0))]
    unnamed x11 -> x3, local copies, waits for them, and re-layouts: 5.74 us -> 5.21 us
  transfers between devices with their start and end apart: 2 -> 0, of which waited for: 0 -> 0; matrix products, arithmetic and copies ran while one was open for 4% -> 0% of each run, Pallas kernels for 0% -> 0%
where the time goes in v3:
time: 117 us; the launch traced here: 115 us
  Pallas kernels  106 us (91%)
  local copies, waits for them, and re-layouts  6.68 us (6%)
  other arithmetic  2.16 us (2%)
    pallas_call x1, Pallas kernels, run_step(): pl.pallas_call(step_kernel, in_specs=[pl.BlockSpec(memory_space=pltpu.SME...  106 us
    unnamed x3, local copies, waits for them, and re-layouts  5.21 us

profile of v3, /device:TPU:7, one launch (start us, length us, event | category | flops | bytes accessed | tf_op | source)
XLA Modules:
  0.0 115.4 jit_solution(2309951233137734879)
XLA Ops:
  0.7 0.1 stack.36
  0.8 0.1 stack.42
  0.9 0.9 compare_reduce_fusion
  1.7 0.6 broadcast_select_fusion.bias_ref
  2.3 0.7 convert_element_type.3
  3.0 0.1 broadcast_in_dim.33
  3.1 0.6 broadcast_in_dim.34.freq_ref
  3.7 0.6 broadcast_in_dim.32.spots_ref
  4.3 105.9 %whole_step.1 = (bf16[256,1024]{1,0:T(8,128)(2,1)}, bf16[256,1024]{1,0:T(8,128)(2,1)}, f32[64,192]{1,0:T(8,128)}) custom-call(f32[2,5]{1,0:T(2,128)} %broadcast_select_fusion.bias_ref, bf16[256,1024]{1,0:T(8,128)(2,1)} %bitcast.17, bf16[1024,3072]{1,0:T(8,128)(2,1)} %w_hbm.1, bf16[256,1024]{1,0:T(8,128)(2,1)} %bitcast.18, ...), custom_call_target="tpu_custom_call" | custom-call | tf_op jit(solution)/shard_map/whole_step/pallas_call | solution.py:435
  110.2 1.9 %copy.11 = bf16[1,256,1024]{2,1,0:T(8,128)(2,1)} copy(bf16[1,256,1024]{2,1,0:T(8,128)(2,1)} %bitcast.16) | data formatting | bytes 1048576
  112.0 1.9 %copy.12 = bf16[1,256,1024]{2,1,0:T(8,128)(2,1)} copy(bf16[1,256,1024]{2,1,0:T(8,128)(2,1)} %bitcast.15) | data formatting | bytes 1048576
  113.9 1.5 %copy.13 = f32[64,192]{1,0:T(8,128)} copy(f32[64,192]{1,0:T(8,128)} %get-tuple-element.14) | data formatting | bytes 98304
  (4 shorter events, 0.0 us)

commit v4 on v3

v4 whole, which is shorter than its diff:
```python
import jax
import jax.numpy as jnp
import numpy as np
from jax import lax
from jax.experimental import pallas as pl
from jax.experimental.pallas import tpu as pltpu
from jax.sharding import PartitionSpec as P

INTERP = 0.25
BASE = 10000.0
FAR = 1e30
LOG2E = 1.4426950408889634
BF = jnp.bfloat16
F32 = jnp.float32
MESH = pl.DeviceIdType.MESH
ROWS = 256
GROUPS = 4
SLOTS = 5
PIECES = 4


def dot(a, b):
    return lax.dot_general(a, b, (((1,), (0,)), ((), ())), preferred_element_type=F32)


def dot_t(a, b):
    return lax.dot_general(a, b, (((1,), (1,)), ((), ())), preferred_element_type=F32)


def lanes(shape):
    return lax.broadcasted_iota(jnp.int32, shape, len(shape) - 1)


def perm_matrix():
    source = lax.broadcasted_iota(jnp.int32, (256, 256), 0)
    column = lax.broadcasted_iota(jnp.int32, (256, 256), 1)
    wanted = (column // 32 % 4) * 64 + (column // 128) * 32 + column % 32
    return jnp.where(source == wanted, 1.0, 0.0).astype(BF)


def turn(value, cosine, sine):
    a, c = value[:, :128], value[:, 128:]
    return jnp.concatenate([a * cosine - c * sine, a * sine + c * cosine], axis=1)


def turn_back(value, cosine, sine):
    a, c = value[:, :128], value[:, 128:]
    return jnp.concatenate([a * cosine + c * sine, c * cosine - a * sine], axis=1)


def step_kernel(list_ref, x_hbm, w_hbm, up_hbm, spots_ref, freq_ref,
                out_hbm, gx_hbm, gw_ref,
                out_ref, gx_ref,
                perm_ref, xs, spots, wbuf, wpair, upbuf, qbuf, kbuf, vbuf, cos5, sin5, stats, both, xt,
                g_buf, in_x, in_y, sum_a, sum_b, in_a, in_b, sum_p, in_z,
                local, x_send, x_recv, p_send, p_recv, u_send, u_recv, s_send, s_recv, d_send, d_recv,
                send_x, recv_x, send_y, recv_y, send_a, recv_a, send_b, recv_b, send_z, recv_z):
    lon, dates = lax.axis_index("lon"), lax.axis_index("dates")
    x, y_lo, core = lon // 4, lax.rem(lon // 2, 2), lax.rem(lon, 2)
    z, y_hi = dates // 2, lax.rem(dates, 2)
    y = y_hi * 2 + y_lo
    step = 1 - 2 * y_lo

    def at(px, py, pz, pc):
        return {"lon": lax.rem(px + 4, 4) * 4 + lax.rem(py, 2) * 2 + pc, "dates": pz * 2 + py // 2}

    other_y = y_hi * 2 + 1 - y_lo
    partner = at(x, y, z, 1 - core)
    pair = at(x, other_y, z, core)
    onward = at(x + step, y, z, core)
    diagonal = at(x - step, other_y, z, core)
    passing = 2 + lax.rem(core + y_lo, 2)
    x_peers = [lax.rem(x + i, 4) for i in (1, 2, 3)]
    y_peers = [lax.rem(y + i, 4) for i in (1, 2, 3)]
    z_peers = [lax.rem(z + i, 8) for i in range(1, 8)]

    bring = [pltpu.make_async_copy(x_hbm, xs.at[0], local.at[0]),
             pltpu.make_async_copy(w_hbm, wbuf, local.at[1]),
             pltpu.make_async_copy(up_hbm, upbuf.at[pl.ds(0, ROWS)], local.at[2])]
    for copy in bring:
        copy.start()
    barrier = pltpu.get_barrier_semaphore()
    peers = [partner, diagonal] + [at(p, y, z, core) for p in x_peers] + [at(x, p, z, core) for p in y_peers]
    peers += [at(x, y, p, c) for p in z_peers for c in range(2)]
    for peer in peers:
        pl.semaphore_signal(barrier, inc=1, device_id=peer, device_id_type=MESH)
    pl.semaphore_wait(barrier, len(peers))

    offsets = (0, 1 - 2 * core, 2 * step, -2 * step, 2 * core - 1)

    def bias(offset):
        found = list_ref[0, 0] == offset
        for i in range(1, 5):
            found = jnp.logical_or(found, list_ref[0, i] == offset)
        return jnp.where(found, 0.0, FAR)

    bias_to = [bias(offset) for offset in offsets]
    bias_from = [bias(-offset) for offset in offsets]

    def remote(source, target, send_sem, recv_sem, peer):
        return pltpu.make_async_remote_copy(src_ref=source, dst_ref=target, send_sem=send_sem, recv_sem=recv_sem,
                                            device_id=peer, device_id_type=MESH)

    routes = ((1, partner), (2, pair), (3, diagonal))
    p_copies = {slot: remote(spots_ref, spots.at[slot], p_send.at[slot], p_recv.at[slot], peer) for slot, peer in routes}
    p_copies[4] = remote(spots.at[passing], spots.at[4], p_send.at[4], p_recv.at[4], partner)

    def piece(j):
        return pl.ds(j * (ROWS // PIECES), ROWS // PIECES)

    x_partner = remote(x_hbm, xs.at[1], x_send.at[0], x_recv.at[0], partner)
    x_pair = [remote(x_hbm.at[piece(j)], xs.at[2, piece(j)], x_send.at[2 + j], x_recv.at[2 + j], pair)
              for j in range(PIECES)]
    x_cross = [remote(xs.at[2, piece(j)], xs.at[3, piece(j)], x_send.at[2 + PIECES + j], x_recv.at[2 + PIECES + j], onward)
               for j in range(PIECES)]
    x_pass = [remote(xs.at[passing, piece(j)], xs.at[4, piece(j)], x_send.at[2 + 2 * PIECES + j],
                     x_recv.at[2 + 2 * PIECES + j], partner) for j in range(PIECES)]

    def block(slot):
        return pl.ds(pl.multiple_of(slot * ROWS, ROWS), ROWS)

    def block_piece(slot, j):
        return pl.ds(slot * ROWS + j * (ROWS // PIECES), ROWS // PIECES)

    u_partner = remote(up_hbm, upbuf.at[block(1)], u_send.at[0], u_recv.at[0], partner)
    u_pass = remote(upbuf.at[block(passing)], upbuf.at[block(4)], u_send.at[1], u_recv.at[1], partner)
    u_pair = [remote(up_hbm.at[piece(j)], upbuf.at[block_piece(2, j)], u_send.at[2 + j], u_recv.at[2 + j], pair)
              for j in range(PIECES)]
    u_cross = [remote(upbuf.at[block_piece(2, j)], upbuf.at[block_piece(3, j)], u_send.at[2 + PIECES + j],
                      u_recv.at[2 + PIECES + j], onward) for j in range(PIECES)]
    for slot in (1, 2, 3):
        p_copies[slot].start()
    for copy in x_pair:
        copy.start()
    x_partner.start()
    for copy in u_pair:
        copy.start()
    u_partner.start()

    perm_ref[...] = perm_matrix()
    bring[0].wait()
    bring[1].wait()

    def cols(part, g):
        return pl.ds(pl.multiple_of(part * 1024 + g * 256, 256), 256)

    @pl.loop(0, 2 * GROUPS)
    def _(g):
        wpair[:, cols(0, g)] = dot(wbuf[:, cols(0, g)], perm_ref[...]).astype(BF)

    def tables(slot, row):
        spread = jnp.broadcast_to(row.astype(F32), (128, ROWS)).T
        angle = spread * freq_ref[0:1, :]
        cos5[slot] = jnp.cos(angle)
        sin5[slot] = jnp.sin(angle)

    def project(slot):
        into = block(slot)

        @pl.loop(0, GROUPS)
        def _(g):
            tokens = xs[slot]
            cosine, sine = cos5[slot], sin5[slot]
            query = turn(dot(tokens, wpair[:, cols(0, g)]), cosine, sine).astype(BF).astype(F32) * 0.125
            qbuf[into, cols(0, g)] = query.astype(BF)
            kbuf[into, cols(0, g)] = turn(dot(tokens, wpair[:, cols(1, g)]), cosine, sine).astype(BF)
            vbuf[into, cols(0, g)] = dot(tokens, wbuf[:, cols(2, g)]).astype(BF)

    def hand_on(j):
        x_pair[j].wait_recv()
        x_cross[j].start()

    def stripes(slot):
        row = lax.broadcasted_iota(jnp.int32, (128, 256), 0)
        chosen = lanes((128, 256)) == row // 32 * 64 + core * 32 + row % 32
        select = jnp.where(chosen, 1.0, 0.0).astype(BF)
        for g in range(GROUPS):
            xt[g * 128:(g + 1) * 128, slot * ROWS:(slot + 1) * ROWS] = dot_t(select, xs[slot, :, g * 256:(g + 1) * 256]).astype(BF)

    def hand_on_up(j):
        u_pair[j].wait_recv()
        u_cross[j].start()

    tables(0, spots_ref[...])
    hand_on(0)
    project(0)
    hand_on(1)
    p_copies[1].wait()
    tables(1, spots[1])
    x_partner.wait()
    project(1)
    hand_on(2)
    p_copies[2].wait()
    p_copies[3].wait()
    p_copies[4].start()
    tables(2, spots[2])
    tables(3, spots[3])
    hand_on(3)
    project(2)
    p_copies[4].wait()
    tables(4, spots[4])
    stripes(0)
    stripes(1)
    for cross, passed in zip(x_cross, x_pass):
        cross.wait_recv()
        passed.start()
    project(3)
    hand_on_up(0)
    bring[2].wait()
    for copy in x_pass:
        copy.wait_recv()
    project(4)
    hand_on_up(1)
    lane = lanes((ROWS, 256))
    lane_pair = lane // 32 % 4
    lane_flat = lane // 64
    stat_lane = lanes((ROWS, 128))
    zero = jnp.zeros((), BF)

    def s_copy(g, slot, peer):
        return remote(stats.at[passing if slot == 4 else 0, g], stats.at[slot, g],
                      s_send.at[slot, g], s_recv.at[slot, g], peer)

    def d_copy(part, g):
        return remote(both.at[pl.ds(0, ROWS), cols(part, g)], both.at[pl.ds(ROWS, ROWS), cols(part, g)],
                      d_send.at[part, g], d_recv.at[part, g], partner)

    def send_first(s):
        px, lo = s // 6, lax.rem(s // 3, 2)

        @pl.when(px != x)
        def _():
            slot = lax.rem(px - x + 3, 4)
            remote(g_buf.at[s, pl.ds(0, 4)], in_x.at[slot, s - 6 * px], send_x.at[slot], recv_x.at[slot],
                   at(px, y, z, core)).start()

        for hi in range(2):
            py = hi * 2 + lo

            @pl.when(py != y)
            def _():
                slot = lax.rem(py - y + 3, 4)
                remote(g_buf.at[s, pl.ds(4, 4), hi], in_y.at[slot, px * 3 + lax.rem(s, 3)], send_y.at[slot],
                       recv_y.at[slot], at(x, py, z, core)).start()

    def weight_piece(part, g):
        d_copy(part, g).wait_recv()
        value = dot(xt[...], both[:, cols(part, g)]).astype(BF)
        first = part * 8 + g * 2
        g_buf[first] = value[:, :128].reshape(8, 2, 32, 128)
        g_buf[first + 1] = value[:, 128:].reshape(8, 2, 32, 128)
        send_first(first)
        send_first(first + 1)

    def pass_stats(g):
        s_copy(g, 2, pair).wait_recv()
        s_copy(g, 3, diagonal).wait_recv()
        s_copy(g, 4, partner).start()

    def out_copy(g):
        return pltpu.make_async_copy(out_ref.at[:, cols(0, g)], out_hbm.at[:, cols(0, g)], local.at[3 + g])

    @pl.loop(0, GROUPS)
    def _(g):
        mid = cols(0, g)
        query = qbuf[block(0), mid]
        up_g = upbuf[block(0), mid]
        out = jnp.zeros((ROWS, 256), F32)
        dquery = jnp.zeros((ROWS, 256), F32)
        now = jnp.zeros((ROWS, 128), F32)
        for head in range(4):
            own_pair = lane_pair == head
            own_flat = lane_flat == head
            scores = dot_t(jnp.where(own_pair, query, zero), kbuf[:, mid])
            row_max = None
            for slot in range(SLOTS):
                left = slot * ROWS
                one = jnp.maximum(scores[:, left:left + 128], scores[:, left + 128:left + 256]) - bias_to[slot]
                row_max = one if row_max is None else jnp.maximum(row_max, one)
            row_max = jnp.max(row_max, axis=1, keepdims=True)
            parts = []
            total = None
            for slot in range(SLOTS):
                one = jnp.exp2((scores[:, slot * ROWS:(slot + 1) * ROWS] - (row_max + bias_to[slot])) * LOG2E)
                part_sum = one[:, :128] + one[:, 128:]
                total = part_sum if total is None else total + part_sum
                parts.append(one)
            total = jnp.sum(total, axis=1, keepdims=True)
            weights = jnp.concatenate(parts, axis=1)
            inverse = 1.0 / total
            attended = dot(weights.astype(BF), vbuf[:, mid]) * inverse
            attended = attended.astype(BF).astype(F32)
            out = jnp.where(own_flat, attended, out)
            up_own = jnp.where(own_flat, up_g, zero)
            delta = jnp.sum(up_own.astype(F32) * attended, axis=1, keepdims=True)
            dprobs = dot_t(up_own, vbuf[:, mid])
            dscores = (weights * (dprobs - delta)).astype(BF)
            dquery = jnp.where(own_pair, dot(dscores, kbuf[:, mid]) * (inverse * 0.125), dquery)
            now = jnp.where(stat_lane == head, row_max * LOG2E + jnp.log2(total), now)
            now = jnp.where(stat_lane == head + 4, delta, now)
        stats[0, g] = now.T[:8]
        dquery = turn_back(dquery, cos5[0], sin5[0]).astype(BF)
        both[0:ROWS, mid] = dot_t(dquery, perm_ref[...]).astype(BF)
        out_ref[:, mid] = out.astype(BF)
        for slot, peer in routes:
            s_copy(g, slot, peer).start()
        d_copy(0, g).start()
        out_copy(g).start()

        @pl.when(g == 0)
        def _():
            hand_on_up(2)
            hand_on_up(3)

        @pl.when(g == 2)
        def _():
            for copy in u_cross:
                copy.wait_recv()
            u_pass.start()

        @pl.when(g > 0)
        def _():
            pass_stats(g - 1)
            weight_piece(0, g - 1)

    def gx_copy(j):
        return pltpu.make_async_copy(gx_ref.at[:, pl.ds(j * 256, 256)], gx_hbm.at[:, pl.ds(j * 256, 256)], local.at[7 + j])

    def grad_x(j):
        rows = slice(j * 256, (j + 1) * 256)
        gx_ref[:, rows] = dot_t(both[0:ROWS], wbuf[rows]).astype(BF)
        gx_copy(j).start()

    @pl.loop(0, GROUPS)
    def _(g):
        mid = cols(0, g)
        s_copy(g, 1, partner).wait_recv()
        s_copy(g, 4, partner).wait_recv()

        @pl.when(g == 0)
        def _():
            u_partner.wait_recv()
            u_pass.wait_recv()

        key, value = kbuf[block(0), mid], vbuf[block(0), mid]
        dkey = jnp.zeros((ROWS, 256), F32)
        dvalue = jnp.zeros((ROWS, 256), F32)
        for head in range(4):
            own_pair = lane_pair == head
            own_flat = lane_flat == head
            lse = jnp.concatenate([stats[slot, g, head:head + 1] + bias_from[slot] for slot in range(SLOTS)], axis=1)
            delta = jnp.concatenate([stats[slot, g, head + 4:head + 5] for slot in range(SLOTS)], axis=1)
            scores = dot_t(jnp.where(own_pair, key, zero), qbuf[:, mid]) * LOG2E
            probs = jnp.exp2(scores - lse)
            dprobs = dot_t(jnp.where(own_flat, value, zero), upbuf[:, mid])
            dscores = (probs * (dprobs - delta)).astype(BF)
            dvalue = jnp.where(own_flat, dot(probs.astype(BF), upbuf[:, mid]), dvalue)
            dkey = jnp.where(own_pair, dot(dscores, qbuf[:, mid]), dkey)
            if head == 2:
                @pl.when(g == 0)
                def _():
                    pass_stats(GROUPS - 1)
                    weight_piece(0, GROUPS - 1)

                @pl.when(g > 0)
                def _():
                    weight_piece(2, g - 1)
                    weight_piece(1, g - 1)
        dkey = turn_back(dkey, cos5[0], sin5[0]).astype(BF)
        both[0:ROWS, cols(2, g)] = dvalue.astype(BF)
        both[0:ROWS, cols(1, g)] = dot_t(dkey, perm_ref[...]).astype(BF)
        d_copy(2, g).start()
        d_copy(1, g).start()

    grad_x(0)
    weight_piece(2, GROUPS - 1)
    weight_piece(1, GROUPS - 1)

    grad_x(1)
    first_a = [remote(in_x.at[i], in_x.at[i], send_x.at[i], recv_x.at[i], at(p, y, z, core)) for i, p in enumerate(x_peers)]
    first_b = [remote(in_y.at[i], in_y.at[i], send_y.at[i], recv_y.at[i], at(x, p, z, core)) for i, p in enumerate(y_peers)]
    for copy in first_a:
        copy.wait_recv()
    for j in range(6):
        total = g_buf[6 * x + j, 0:4].astype(F32)
        for i in range(3):
            total += in_x[i, j].astype(F32)
        sum_a[j] = total.astype(BF)
    second_a = [remote(sum_a.at[pl.ds(lax.rem(p, 2) * 3, 3), :, p // 2], in_a.at[i], send_a.at[i], recv_a.at[i],
                       at(x, p, z, core)) for i, p in enumerate(y_peers)]
    for copy in second_a:
        copy.start()
    for copy in first_b:
        copy.wait_recv()
    for px in range(4):
        for j in range(3):
            total = g_buf[px * 6 + y_lo * 3 + j, 4:8, y_hi].astype(F32)
            for i in range(3):
                total += in_y[i, px * 3 + j].astype(F32)
            sum_b[px * 3 + j] = total.astype(BF)
    second_b = [remote(sum_b.at[pl.ds(p * 3, 3)], in_b.at[i], send_b.at[i], recv_b.at[i], at(p, y, z, core))
                for i, p in enumerate(x_peers)]
    for copy in second_b:
        copy.start()
    grad_x(2)
    for copy in second_a:
        copy.wait_recv()
    def halves(rows, blocks):
        middle = blocks[1].astype(BF).astype(F32)
        for c in range(2):
            part = middle[:, :, c * 64:(c + 1) * 64]
            sum_p[rows, c, 0:32] = blocks[2 * c].astype(BF)
            sum_p[rows, c, 32:48] = jnp.concatenate([part[:, :16], part[:, 16:]], axis=2).astype(BF)

    third = [(z, remote(sum_p.at[z, 1 - core], in_z.at[0, core], send_z.at[0, 1 - core], recv_z.at[0, core], partner))]
    for i, p in enumerate(z_peers):
        for c in range(2):
            third.append((p, remote(sum_p.at[p, c], in_z.at[i + 1, core], send_z.at[i + 1, c], recv_z.at[i + 1, core],
                                    at(x, y, p, c))))

    def send_third(upper):
        for p, copy in third:
            @pl.when(p // 4 == upper)
            def _():
                copy.start()

    blocks = []
    for j in range(3):
        total = sum_a[y_lo * 3 + j, :, y_hi].astype(F32)
        for i in range(3):
            total += in_a[i, j].astype(F32)
        blocks.append(total)
    halves(slice(0, 4), blocks)
    send_third(0)
    for copy in second_b:
        copy.wait_recv()
    blocks = []
    for j in range(3):
        total = sum_b[x * 3 + j].astype(F32)
        for i in range(3):
            total += in_b[i, j].astype(F32)
        blocks.append(total)
    halves(slice(4, 8), blocks)
    send_third(1)
    grad_x(3)
    for copy in first_a + first_b + second_a + second_b + x_pair + x_cross + x_pass + u_pair + u_cross + [u_partner, u_pass]:
        copy.wait_send()

    @pl.loop(0, GROUPS)
    def _(g):
        for part in range(3):
            d_copy(part, g).wait_send()
        s_copy(g, 1, partner).wait_send()
        s_copy(g, 2, pair).wait_send()
        s_copy(g, 3, diagonal).wait_send()
        s_copy(g, 4, partner).wait_send()
        out_copy(g).wait()

    for j in range(4):
        gx_copy(j).wait()
    for _, copy in third:
        copy.wait_send()

    def arrived(i, c):
        remote(in_z.at[i, c], in_z.at[i, c], send_z.at[i, c], recv_z.at[i, c], partner).wait_recv()

    for own in (False, True):
        c = core if own else 1 - core
        total = None
        for i in range(8):
            if own and i == 0:
                one = sum_p[z, core]
            else:
                arrived(i, c)
                one = in_z[i, c]
            total = one.astype(F32) if total is None else total + one.astype(F32)
        total = total * (65536.0 ** -0.5)
        whole = total[:32]
        middle = jnp.concatenate([total[32:, :64], total[32:, 64:]], axis=0)
        gw_ref[pl.ds(pl.multiple_of(c * 32, 32), 32), :] = jnp.where(
            core == 0, jnp.concatenate([whole, middle], axis=1), jnp.concatenate([middle, whole], axis=1))


def run_step(listed, x, w, up, spots, freq):
    vmem = pl.BlockSpec(memory_space=pltpu.VMEM)
    hbm = pl.BlockSpec(memory_space=pl.ANY)
    dma = pltpu.SemaphoreType.DMA
    block = jax.ShapeDtypeStruct((ROWS, 1024), BF)
    buffers = [
        ((ROWS, 1024), BF), ((ROWS, 1024), BF),
        ((256, 256), BF), ((SLOTS, ROWS, 1024), BF), ((SLOTS, 1, ROWS), jnp.int32), ((1024, 3072), BF), ((1024, 2048), BF),
        ((SLOTS * ROWS, 1024), BF), ((SLOTS * ROWS, 1024), BF), ((SLOTS * ROWS, 1024), BF), ((SLOTS * ROWS, 1024), BF),
        ((SLOTS, ROWS, 128), F32), ((SLOTS, ROWS, 128), F32), ((SLOTS, GROUPS, 8, ROWS), F32),
        ((2 * ROWS, 3072), BF), ((512, 512), BF),
        ((24, 8, 2, 32, 128), BF), ((3, 6, 4, 2, 32, 128), BF), ((3, 12, 4, 32, 128), BF), ((6, 4, 2, 32, 128), BF),
        ((12, 4, 32, 128), BF), ((3, 3, 4, 32, 128), BF), ((3, 3, 4, 32, 128), BF), ((8, 2, 48, 128), BF),
        ((8, 2, 48, 128), BF),
    ]
    x_moves, u_moves = (2 + 3 * PIECES,), (2 + 2 * PIECES,)
    semaphores = [dma((11,)), dma(x_moves), dma(x_moves), dma((5,)), dma((5,)), dma(u_moves), dma(u_moves)]
    semaphores += [dma((5, GROUPS))] * 2 + [dma((3, GROUPS))] * 2 + [dma((3,))] * 8 + [dma((8, 2))] * 2
    return pl.pallas_call(
        step_kernel,
        in_specs=[pl.BlockSpec(memory_space=pltpu.SMEM), hbm, hbm, hbm, vmem, vmem],
        out_specs=[hbm, hbm, vmem],
        out_shape=[block, block, jax.ShapeDtypeStruct((64, 192), F32)],
        scratch_shapes=[pltpu.VMEM(shape, kind) for shape, kind in buffers] + semaphores,
        compiler_params=pltpu.CompilerParams(collective_id=0, has_side_effects=True, vmem_limit_bytes=63 * 2**20),
        name="whole_step",
    )(listed, x, w, up, spots, freq)


def hand_out_kernel(a_hbm, b_hbm, c_hbm, a_out, b_out, c_out, a_buf, b_buf, c_buf, sems):
    moves = []
    for source, buffer, target, parts in ((a_hbm, a_buf, a_out, 4), (b_hbm, b_buf, b_out, 4), (c_hbm, c_buf, c_out, 1)):
        rows = buffer.shape[0] // parts
        for i in range(parts):
            part = pl.ds(i * rows, rows)
            sem = sems.at[len(moves)]
            moves.append((pltpu.make_async_copy(source.at[part], buffer.at[part], sem),
                          pltpu.make_async_copy(buffer.at[part], target.at[part], sem)))
    for bring, _ in moves:
        bring.start()
    for bring, give in moves:
        bring.wait()
        give.start()
    for _, give in moves:
        give.wait()


def hand_out(a, b, c):
    hbm = pl.BlockSpec(memory_space=pl.ANY)
    arrays = (a, b, c)
    return pl.pallas_call(
        hand_out_kernel,
        in_specs=[hbm] * 3,
        out_specs=[hbm] * 3,
        out_shape=[jax.ShapeDtypeStruct(one.shape, one.dtype) for one in arrays],
        scratch_shapes=[pltpu.VMEM(one.shape, one.dtype) for one in arrays] + [pltpu.SemaphoreType.DMA((9,))],
        name="hand_out",
    )(*arrays)


def per_device(features, w_qkv, grad_out, positions, block_list):
    frequency = np.float32(INTERP) * np.float32(BASE) ** (np.float32(-2.0) * np.arange(32, dtype=np.float32) / np.float32(64))
    freq = jnp.asarray(np.broadcast_to(np.tile(frequency, 4), (8, 128)))
    out, grad_x, grad_w = hand_out(*run_step(block_list, features[0], w_qkv, grad_out[0], positions, freq))
    return (out[None], grad_x[None], grad_w)


def solution(mesh):
    return jax.shard_map(
        per_device,
        mesh=mesh,
        in_specs=(
            P("dates", "lon", None),
            P(),
            P("dates", "lon", None),
            P("dates", "lon"),
            P("dates", None),
        ),
        out_specs=(P("dates", "lon", None), P("dates", "lon", None), P("dates", "lon")),
        check_vma=False,
    )
```

time: 117 us -> 104 us (0.89)
  local copies, waits for them, and re-layouts: 6.68 us -> 1.25 us
  Pallas kernels: 106 us -> 101 us
  other arithmetic: 2.16 us -> 0 us
    pallas_call x1, Pallas kernels: 106 us -> 99.4 us  [run_step(): pl.pallas_call(step_kernel, in_specs=[pl.BlockSpec(memory_space=pltpu.SME...]
    unnamed x3 -> x0, local copies, waits for them, and re-layouts: 5.21 us -> none
    pallas_call x0 -> x1, Pallas kernels: none -> 2.04 us  [hand_out(): pl.pallas_call(hand_out_kernel, in_specs=[hbm] * 3, out_specs=[hbm] * 3,...]
    broadcast_in_dim x3 -> x0, local copies, waits for them, and re-layouts: 1.28 us -> none  [the longest x2 0.68 us: per_device(): freq = jnp.broadcast_to(jnp.tile(frequency, 4)[None], (8, 128))]
where the time goes in v4:
time: 104 us
  Pallas kernels  101 us (97%)
  local copies, waits for them, and re-layouts  1.25 us (1%)
    pallas_call x1, Pallas kernels, run_step(): pl.pallas_call(step_kernel, in_specs=[pl.BlockSpec(memory_space=pltpu.SME...  99.4 us

profile of v4, /device:TPU:7, one launch (start us, length us, event | category | flops | bytes accessed | tf_op | source)
XLA Modules:
  0.0 103.5 jit_solution(8112130015220267381)
XLA Ops:
  0.6 1.3 %jit_solution_.3.freq_ref = f32[8,128]{1,0:T(8,128)} broadcast(f32[128]{0:T(128)} %constant.2.clone), dimensions={1} | broadcast | bytes 4608 | tf_op jit(solution)
  1.9 99.4 %whole_step.1 = (bf16[256,1024]{1,0:T(8,128)(2,1)}, bf16[256,1024]{1,0:T(8,128)(2,1)}, f32[64,192]{1,0:T(8,128)}) custom-call(s32[1,5]{1,0:T(1,128)} %list_ref.1, bf16[256,1024]{1,0:T(8,128)(2,1)} %bitcast.4, bf16[1024,3072]{1,0:T(8,128)(2,1)} %w_hbm.1, bf16[256,1024]{1,0:T(8,128)(2,1)} %bitcast.5, s32[1,256]{1,0:T(1,128)} %spots_ref.1, ...), custom_call_target="tpu_custom_call" | custom-call | tf_op jit(solution)/shard_map/whole_step/pallas_call | solution.py:502
  101.3 2.0 %hand_out.1 = (bf16[256,1024]{1,0:T(8,128)(2,1)}, bf16[256,1024]{1,0:T(8,128)(2,1)}, f32[64,192]{1,0:T(8,128)}) custom-call(bf16[256,1024]{1,0:T(8,128)(2,1)} %get-tuple-element.9.a_hbm, bf16[256,1024]{1,0:T(8,128)(2,1)} %get-tuple-element.10.b_hbm, f32[64,192]{1,0:T(8,128)} %get-tuple-element.11.c_hbm), custom_call_target="tpu_custom_call" | custom-call | tf_op jit(solution)/shard_map/hand_out/pallas_call | solution.py:534

commit v5 on v4

--- a/solution.py
+++ b/solution.py
@@ -10,6 +10,7 @@
 BASE = 10000.0
 FAR = 1e30
 LOG2E = 1.4426950408889634
+FREQUENCY = [float(np.float32(INTERP) * np.float32(BASE) ** np.float32(-2.0 * j / 64)) for j in range(32)]
 BF = jnp.bfloat16
 F32 = jnp.float32
 MESH = pl.DeviceIdType.MESH
@@ -48,9 +49,9 @@
     return jnp.concatenate([a * cosine + c * sine, c * cosine - a * sine], axis=1)
 
 
-def step_kernel(list_ref, x_hbm, w_hbm, up_hbm, spots_ref, freq_ref,
-                out_hbm, gx_hbm, gw_ref,
-                out_ref, gx_ref,
+def step_kernel(list_hbm, x_hbm, w_hbm, up_hbm, spots_hbm,
+                out_hbm, gx_hbm, gw_hbm,
+                list_ref, out_ref, gx_ref, gw_ref,
                 perm_ref, xs, spots, wbuf, wpair, upbuf, qbuf, kbuf, vbuf, cos5, sin5, stats, both, xt,
                 g_buf, in_x, in_y, sum_a, sum_b, in_a, in_b, sum_p, in_z,
                 local, x_send, x_recv, p_send, p_recv, u_send, u_recv, s_send, s_recv, d_send, d_recv,
@@ -76,7 +77,9 @@
 
     bring = [pltpu.make_async_copy(x_hbm, xs.at[0], local.at[0]),
              pltpu.make_async_copy(w_hbm, wbuf, local.at[1]),
-             pltpu.make_async_copy(up_hbm, upbuf.at[pl.ds(0, ROWS)], local.at[2])]
+             pltpu.make_async_copy(up_hbm, upbuf.at[pl.ds(0, ROWS)], local.at[2]),
+             pltpu.make_async_copy(spots_hbm, spots.at[0], local.at[11]),
+             pltpu.make_async_copy(list_hbm, list_ref, local.at[12])]
     for copy in bring:
         copy.start()
     barrier = pltpu.get_barrier_semaphore()
@@ -94,15 +97,12 @@
             found = jnp.logical_or(found, list_ref[0, i] == offset)
         return jnp.where(found, 0.0, FAR)
 
-    bias_to = [bias(offset) for offset in offsets]
-    bias_from = [bias(-offset) for offset in offsets]
-
     def remote(source, target, send_sem, recv_sem, peer):
         return pltpu.make_async_remote_copy(src_ref=source, dst_ref=target, send_sem=send_sem, recv_sem=recv_sem,
                                             device_id=peer, device_id_type=MESH)
 
     routes = ((1, partner), (2, pair), (3, diagonal))
-    p_copies = {slot: remote(spots_ref, spots.at[slot], p_send.at[slot], p_recv.at[slot], peer) for slot, peer in routes}
+    p_copies = {slot: remote(spots_hbm, spots.at[slot], p_send.at[slot], p_recv.at[slot], peer) for slot, peer in routes}
     p_copies[4] = remote(spots.at[passing], spots.at[4], p_send.at[4], p_recv.at[4], partner)
 
     def piece(j):
@@ -148,9 +148,14 @@
     def _(g):
         wpair[:, cols(0, g)] = dot(wbuf[:, cols(0, g)], perm_ref[...]).astype(BF)
 
+    pair_index = lax.rem(lanes((1, 128)), 32)
+    frequency = jnp.zeros((1, 128), F32)
+    for j, one in enumerate(FREQUENCY):
+        frequency = jnp.where(pair_index == j, one, frequency)
+
     def tables(slot, row):
         spread = jnp.broadcast_to(row.astype(F32), (128, ROWS)).T
-        angle = spread * freq_ref[0:1, :]
+        angle = spread * frequency
         cos5[slot] = jnp.cos(angle)
         sin5[slot] = jnp.sin(angle)
 
@@ -181,7 +186,11 @@
         u_pair[j].wait_recv()
         u_cross[j].start()
 
-    tables(0, spots_ref[...])
+    bring[3].wait()
+    bring[4].wait()
+    bias_to = [bias(offset) for offset in offsets]
+    bias_from = [bias(-offset) for offset in offsets]
+    tables(0, spots[0])
     hand_on(0)
     project(0)
     hand_on(1)
@@ -331,13 +340,18 @@
         gx_ref[:, rows] = dot_t(both[0:ROWS], wbuf[rows]).astype(BF)
         gx_copy(j).start()
 
+    def nth(turn_no):
+        return lax.rem(turn_no + lax.div(turn_no + 2, 3) + lax.div(turn_no, 3), GROUPS)
+
     @pl.loop(0, GROUPS)
-    def _(g):
+    def _(turn_no):
+        g = nth(turn_no)
+        earlier = nth(lax.rem(turn_no + 3, GROUPS))
         mid = cols(0, g)
         s_copy(g, 1, partner).wait_recv()
         s_copy(g, 4, partner).wait_recv()
 
-        @pl.when(g == 0)
+        @pl.when(turn_no == 0)
         def _():
             u_partner.wait_recv()
             u_pass.wait_recv()
@@ -357,15 +371,15 @@
             dvalue = jnp.where(own_flat, dot(probs.astype(BF), upbuf[:, mid]), dvalue)
             dkey = jnp.where(own_pair, dot(dscores, qbuf[:, mid]), dkey)
             if head == 2:
-                @pl.when(g == 0)
+                @pl.when(turn_no == 0)
                 def _():
                     pass_stats(GROUPS - 1)
                     weight_piece(0, GROUPS - 1)
 
-                @pl.when(g > 0)
+                @pl.when(turn_no > 0)
                 def _():
-                    weight_piece(2, g - 1)
-                    weight_piece(1, g - 1)
+                    weight_piece(2, earlier)
+                    weight_piece(1, earlier)
         dkey = turn_back(dkey, cos5[0], sin5[0]).astype(BF)
         both[0:ROWS, cols(2, g)] = dvalue.astype(BF)
         both[0:ROWS, cols(1, g)] = dot_t(dkey, perm_ref[...]).astype(BF)
@@ -373,8 +387,8 @@
         d_copy(1, g).start()
 
     grad_x(0)
-    weight_piece(2, GROUPS - 1)
-    weight_piece(1, GROUPS - 1)
+    weight_piece(2, 1)
+    weight_piece(1, 1)
 
     grad_x(1)
     first_a = [remote(in_x.at[i], in_x.at[i], send_x.at[i], recv_x.at[i], at(p, y, z, core)) for i, p in enumerate(x_peers)]
@@ -464,6 +478,7 @@
     def arrived(i, c):
         remote(in_z.at[i, c], in_z.at[i, c], send_z.at[i, c], recv_z.at[i, c], partner).wait_recv()
 
+    give = []
     for own in (False, True):
         c = core if own else 1 - core
         total = None
@@ -479,15 +494,19 @@
         middle = jnp.concatenate([total[32:, :64], total[32:, 64:]], axis=0)
         gw_ref[pl.ds(pl.multiple_of(c * 32, 32), 32), :] = jnp.where(
             core == 0, jnp.concatenate([whole, middle], axis=1), jnp.concatenate([middle, whole], axis=1))
-
-
-def run_step(listed, x, w, up, spots, freq):
-    vmem = pl.BlockSpec(memory_space=pltpu.VMEM)
+        done = pl.ds(pl.multiple_of(c * 32, 32), 32)
+        give.append(pltpu.make_async_copy(gw_ref.at[done], gw_hbm.at[done], local.at[13 + own]))
+        give[-1].start()
+    for copy in give:
+        copy.wait()
+
+
+def run_step(listed, x, w, up, spots):
     hbm = pl.BlockSpec(memory_space=pl.ANY)
     dma = pltpu.SemaphoreType.DMA
     block = jax.ShapeDtypeStruct((ROWS, 1024), BF)
     buffers = [
-        ((ROWS, 1024), BF), ((ROWS, 1024), BF),
+        ((ROWS, 1024), BF), ((ROWS, 1024), BF), ((64, 192), F32),
         ((256, 256), BF), ((SLOTS, ROWS, 1024), BF), ((SLOTS, 1, ROWS), jnp.int32), ((1024, 3072), BF), ((1024, 2048), BF),
         ((SLOTS * ROWS, 1024), BF), ((SLOTS * ROWS, 1024), BF), ((SLOTS * ROWS, 1024), BF), ((SLOTS * ROWS, 1024), BF),
         ((SLOTS, ROWS, 128), F32), ((SLOTS, ROWS, 128), F32), ((SLOTS, GROUPS, 8, ROWS), F32),
@@ -497,17 +516,17 @@
         ((8, 2, 48, 128), BF),
     ]
     x_moves, u_moves = (2 + 3 * PIECES,), (2 + 2 * PIECES,)
-    semaphores = [dma((11,)), dma(x_moves), dma(x_moves), dma((5,)), dma((5,)), dma(u_moves), dma(u_moves)]
+    semaphores = [dma((15,)), dma(x_moves), dma(x_moves), dma((5,)), dma((5,)), dma(u_moves), dma(u_moves)]
     semaphores += [dma((5, GROUPS))] * 2 + [dma((3, GROUPS))] * 2 + [dma((3,))] * 8 + [dma((8, 2))] * 2
     return pl.pallas_call(
         step_kernel,
-        in_specs=[pl.BlockSpec(memory_space=pltpu.SMEM), hbm, hbm, hbm, vmem, vmem],
-        out_specs=[hbm, hbm, vmem],
+        in_specs=[hbm] * 5,
+        out_specs=[hbm] * 3,
         out_shape=[block, block, jax.ShapeDtypeStruct((64, 192), F32)],
-        scratch_shapes=[pltpu.VMEM(shape, kind) for shape, kind in buffers] + semaphores,
+        scratch_shapes=[pltpu.SMEM((1, 5), jnp.int32)] + [pltpu.VMEM(shape, kind) for shape, kind in buffers] + semaphores,
         compiler_params=pltpu.CompilerParams(collective_id=0, has_side_effects=True, vmem_limit_bytes=63 * 2**20),
         name="whole_step",
-    )(listed, x, w, up, spots, freq)
+    )(listed, x, w, up, spots)
 
 
 def hand_out_kernel(a_hbm, b_hbm, c_hbm, a_out, b_out, c_out, a_buf, b_buf, c_buf, sems):
@@ -542,9 +561,7 @@
 
 
 def per_device(features, w_qkv, grad_out, positions, block_list):
-    frequency = np.float32(INTERP) * np.float32(BASE) ** (np.float32(-2.0) * np.arange(32, dtype=np.float32) / np.float32(64))
-    freq = jnp.asarray(np.broadcast_to(np.tile(frequency, 4), (8, 128)))
-    out, grad_x, grad_w = hand_out(*run_step(block_list, features[0], w_qkv, grad_out[0], positions, freq))
+    out, grad_x, grad_w = hand_out(*run_step(block_list, features[0], w_qkv, grad_out[0], positions))
     return (out[None], grad_x[None], grad_w)
 
 

time: 104 us -> 101 us (0.971)
  local copies, waits for them, and re-layouts: 1.25 us -> 0 us
    pallas_call x1, Pallas kernels: 99.4 us -> 97.9 us  [run_step(): pl.pallas_call(step_kernel, in_specs=[hbm] * 5, out_specs=[hbm] * 3, out_...]
    another operation x1 -> x0, local copies, waits for them, and re-layouts: 1.25 us -> none
where the time goes in v5:
time: 101 us
  Pallas kernels  100 us (99%)
    pallas_call x1, Pallas kernels, run_step(): pl.pallas_call(step_kernel, in_specs=[hbm] * 5, out_specs=[hbm] * 3, out_...  97.9 us
    pallas_call x1, Pallas kernels, hand_out(): pl.pallas_call(hand_out_kernel, in_specs=[hbm] * 3, out_specs=[hbm] * 3,...  2.04 us

profile of v5, /device:TPU:7, one launch (start us, length us, event | category | flops | bytes accessed | tf_op | source)
XLA Modules:
  0.0 100.8 jit_solution(13733907541429321642)
XLA Ops:
  0.6 97.9 %whole_step.1 = (bf16[256,1024]{1,0:T(8,128)(2,1)}, bf16[256,1024]{1,0:T(8,128)(2,1)}, f32[64,192]{1,0:T(8,128)}) custom-call(s32[1,5]{1,0:T(1,128)} %list_hbm.1, bf16[256,1024]{1,0:T(8,128)(2,1)} %bitcast.4, bf16[1024,3072]{1,0:T(8,128)(2,1)} %w_hbm.1, bf16[256,1024]{1,0:T(8,128)(2,1)} %bitcast.5, s32[1,256]{1,0:T(1,128)} %spots_hbm.1), custom_call_target="tpu_custom_call" | custom-call | tf_op jit(solution)/shard_map/whole_step/pallas_call | solution.py:521
  98.6 2.0 %hand_out.1 = (bf16[256,1024]{1,0:T(8,128)(2,1)}, bf16[256,1024]{1,0:T(8,128)(2,1)}, f32[64,192]{1,0:T(8,128)}) custom-call(bf16[256,1024]{1,0:T(8,128)(2,1)} %get-tuple-element.9.a_hbm, bf16[256,1024]{1,0:T(8,128)(2,1)} %get-tuple-element.10.b_hbm, f32[64,192]{1,0:T(8,128)} %get-tuple-element.11.c_hbm), custom_call_target="tpu_custom_call" | custom-call | tf_op jit(solution)/shard_map/hand_out/pallas_call | solution.py:553
